TPU v7x, 32 devices: a whole 2x2x4 slice. The times are simulated.
32 devices in a mesh: gx: 16 (over z, y, core), gy: 2 (over x).
Axes of the slice: x: 2, y: 2, z: 4, core: 2. Of those that a mesh axis runs over, the one named last changes fastest.
Arguments:
- populations: float32 [19, 128, 32, 128], P(None, 'gx', 'gy'), may hold values from 0.5 to 2
- ion_density: float32 [2, 128, 32, 128], P(None, 'gx', 'gy'), may hold values from 0.5 to 1.5
- potential: float32 [128, 32, 128], P('gx', 'gy'), may hold values from -6 to 6
- node_flags: int32 [128, 32, 128], P('gx', 'gy'), may hold values from 0 to 64, as said below
- colloid_count: int32 [16, 2], P('gx', 'gy'), may hold values from 0 to 2, as said below
- colloid_centre: int32 [3, 16, 2, 2], P(None, 'gx', 'gy'), may hold values from 0 to 127, as said below
- colloid_velocity: float32 [3, 16, 2, 2], P(None, 'gx', 'gy'), may hold values from -0.5 to 0.5
- colloid_spin: float32 [3, 16, 2, 2], P(None, 'gx', 'gy'), may hold values from -0.1 to 0.1
- bead_cell: int32 [16, 2, 2, 2562], P('gx', 'gy'), may hold values from 0 to 2196
- bead_frac: float32 [3, 16, 2, 2, 2562], P(None, 'gx', 'gy'), may hold values from 0 to 1
- bead_weight: float32 [16, 2, 2, 2562], P('gx', 'gy'), may hold values from 0.25 to 1
Outputs:
- populations_next: float32 [19, 128, 32, 128], P(None, 'gx', 'gy')
- ion_density_next: float32 [2, 128, 32, 128], P(None, 'gx', 'gy')
- potential_next: float32 [128, 32, 128], P('gx', 'gy')
- colloid_kick: float32 [6, 16, 2, 2], P(None, 'gx', 'gy')
Inputs may be any that keep to these rules, and one draw needn't show every extreme that they name: `node_flags`: bits 0 to 5 of a node's flag are 1 where the faces toward -x, +x, -y, +y, -z, +z are open, that is where the node and the neighbour across the face (periodic along all axes) are both fluid; bit 6 marks solid nodes; the nodes at z = 0 and z = 127 are solid; bit 1 of a node equals bit 0 of the next node along x, bit 3 equals bit 2 of the next node along y, bit 5 equals bit 4 of the next node along z. `colloid_count`: slots 0 to count - 1 of a brick hold colloids, the others are to be ignored; some brick has 2. `colloid_centre`: the centre of slot s of brick (i, j) lies in that brick: x in [i * 8, (i + 1) * 8), y in [j * 16, (j + 1) * 16), z in [7, 120].
All inputs are finite; a program needn't handle non-finite values.
Results may differ from a plain program's by a relative error of at most 0.0001.
Values sent between devices are 32-bit elements; how exact they have to be, the bound alone decides.
A program may use at most 128 MiB of HBM per device.

v0:
```python
import jax
import jax.numpy as jnp
import numpy as np
from jax import lax
from jax.sharding import PartitionSpec as P

BEADS = 2562
RADIUS = 6
SWEEPS = 2


LATTICE = np.array(
    [
        [0, 0, 0],
        [1, 0, 0],
        [-1, 0, 0],
        [0, 1, 0],
        [0, -1, 0],
        [0, 0, 1],
        [0, 0, -1],
        [1, 1, 0],
        [-1, -1, 0],
        [1, -1, 0],
        [-1, 1, 0],
        [1, 0, 1],
        [-1, 0, -1],
        [1, 0, -1],
        [-1, 0, 1],
        [0, 1, 1],
        [0, -1, -1],
        [0, 1, -1],
        [0, -1, 1],
    ]
)
OPPOSITE = np.array([0, 2, 1, 4, 3, 6, 5, 8, 7, 10, 9, 12, 11, 14, 13, 16, 15, 18, 17])
PLUS_SETS = [np.array([i for i in range(19) if LATTICE[i][a] == 1]) for a in range(3)]
MINUS_SETS = [np.array([i for i in range(19) if LATTICE[i][a] == -1]) for a in range(3)]
tau_relax = 0.8
kappa_charge = 0.5
friction = 4.0
diffusion = (0.12, 0.15)
valence = (1.0, -1.0)


def padded(block, sides, width):
    for axis, dim in sides:
        count = lax.axis_size(axis)
        forward = [(i, i + 1) for i in range(count - 1)]
        forward.append((count - 1, 0))
        backward = [(target, source) for source, target in forward]
        low = lax.ppermute(
            lax.slice_in_dim(block, block.shape[dim] - width, None, axis=dim), axis, forward
        )
        high = lax.ppermute(lax.slice_in_dim(block, 0, width, axis=dim), axis, backward)
        block = jnp.concatenate([low, block, high], axis=dim)
    return block


def lattice_weight(i):
    if i == 0:
        return 1.0 / 3.0
    if i < 7:
        return 1.0 / 18.0
    return 1.0 / 36.0


def flag_bit(node_flags, bit):
    return (node_flags // 2**bit % 2).astype(jnp.float32)


def moments(pops):
    rows_out = []
    for a in range(3):
        rows_out.append(jnp.sum(pops[PLUS_SETS[a]], 0) - jnp.sum(pops[MINUS_SETS[a]], 0))
    return jnp.stack(rows_out)


def cross_product(left, right):
    return jnp.stack(
        [
            left[1] * right[2] - left[2] * right[1],
            left[2] * right[0] - left[0] * right[2],
            left[0] * right[1] - left[1] * right[0],
        ]
    )


def face_flux(low_ion, high_ion, low_phi, high_phi, low_drift, high_drift, open_face, s):
    middle = 0.5 * (low_ion + high_ion)
    diffusive = -diffusion[s] * (high_ion - low_ion + valence[s] * middle * (high_phi - low_phi))
    return open_face * (diffusive + 0.5 * (low_drift + high_drift) * middle)


def collide(read, density, velocity, force, solid):
    shifted = velocity + tau_relax * force / density
    speed_sq = shifted[0] * shifted[0] + shifted[1] * shifted[1] + shifted[2] * shifted[2]
    results = []
    for i in range(19):
        along_link = jnp.zeros_like(density)
        for a in range(3):
            if LATTICE[i][a] != 0:
                along_link = along_link + float(LATTICE[i][a]) * shifted[a]
        equilibrium = (
            lattice_weight(i)
            * density
            * (1.0 + 3.0 * along_link + 4.5 * along_link * along_link - 1.5 * speed_sq)
        )
        results.append(read[i] - (read[i] - equilibrium) / tau_relax)
    relaxed = jnp.stack(results)
    return jnp.where(solid[None] > 0.5, read[OPPOSITE], relaxed)


def neighbour_sum(wide_field):
    centre_part = wide_field[1:-1, 1:-1]
    z_padded = jnp.pad(centre_part, ((0, 0), (0, 0), (1, 1)))
    return (
        wide_field[2:, 1:-1]
        + wide_field[:-2, 1:-1]
        + wide_field[1:-1, 2:]
        + wide_field[1:-1, :-2]
        + z_padded[:, :, 2:]
        + z_padded[:, :, :-2]
    )


def electric_field(wide_field):
    centre_part = wide_field[1:-1, 1:-1]
    z_padded = jnp.pad(centre_part, ((0, 0), (0, 0), (1, 1)))
    return jnp.stack(
        [
            -(wide_field[2:, 1:-1] - wide_field[:-2, 1:-1]) / 2.0,
            -(wide_field[1:-1, 2:] - wide_field[1:-1, :-2]) / 2.0,
            -(z_padded[:, :, 2:] - z_padded[:, :, :-2]) / 2.0,
        ]
    )


def stream_from(wide_pops, width_x, width_y):
    results = []
    for i in range(19):
        step_x = int(LATTICE[i][0])
        step_y = int(LATTICE[i][1])
        shifted_block = wide_pops[
            i, 1 - step_x : 1 - step_x + width_x, 1 - step_y : 1 - step_y + width_y
        ]
        results.append(jnp.roll(shifted_block, int(LATTICE[i][2]), 2))
    return jnp.stack(results)


def local(
    populations,
    ion_density,
    potential,
    node_flags,
    colloid_count,
    colloid_centre,
    colloid_velocity,
    colloid_spin,
    bead_cell,
    bead_frac,
    bead_weight,
):
    width_x, width_y, depth = potential.shape
    slots = bead_cell.shape[2]
    density_old = jnp.sum(populations, 0)
    drift = moments(populations) / density_old
    charge = ion_density[0] - ion_density[1]
    scalars = jnp.concatenate([ion_density, potential[None], drift], 0)
    wide_pops, wide_scalars = (
        padded(populations, (("gx", 1), ("gy", 2)), 1),
        padded(scalars, (("gx", 1), ("gy", 2)), 1),
    )
    wide_potential = wide_scalars[2]
    for sweep_step in range(SWEEPS):
        relaxed = (neighbour_sum(wide_potential) + kappa_charge * charge) / 6.0
        wide_potential = padded(relaxed, (("gx", 0), ("gy", 1)), 1)
    potential_now = wide_potential[1:-1, 1:-1]
    open_x = jnp.concatenate([flag_bit(node_flags, 0), flag_bit(node_flags, 1)[-1:]], 0)
    open_y = jnp.concatenate([flag_bit(node_flags, 2), flag_bit(node_flags, 3)[:, -1:]], 1)
    open_z = flag_bit(node_flags, 4)
    new_ions = []
    for s in range(2):
        wide_ions = wide_scalars[s]
        ions = wide_ions[1:-1, 1:-1]
        line_ions = wide_ions[:, 1:-1]
        line_phi = wide_potential[:, 1:-1]
        line_drift = wide_scalars[3][:, 1:-1]
        fluxes = face_flux(
            line_ions[:-1],
            line_ions[1:],
            line_phi[:-1],
            line_phi[1:],
            line_drift[:-1],
            line_drift[1:],
            open_x,
            s,
        )
        divergence = jnp.zeros_like(ions) + (fluxes[1:] - fluxes[:-1])
        line_ions = wide_ions[1:-1, :]
        line_phi = wide_potential[1:-1, :]
        line_drift = wide_scalars[4][1:-1, :]
        fluxes = face_flux(
            line_ions[:, :-1],
            line_ions[:, 1:],
            line_phi[:, :-1],
            line_phi[:, 1:],
            line_drift[:, :-1],
            line_drift[:, 1:],
            open_y,
            s,
        )
        divergence = divergence + (fluxes[:, 1:] - fluxes[:, :-1])
        drift_z = drift[2]
        fluxes = face_flux(
            jnp.roll(ions, 1, 2),
            ions,
            jnp.roll(potential_now, 1, 2),
            potential_now,
            jnp.roll(drift_z, 1, 2),
            drift_z,
            open_z,
            s,
        )
        divergence = divergence + (jnp.roll(fluxes, -1, 2) - fluxes)
        new_ions.append(ions - divergence)
    read = stream_from(wide_pops, width_x, width_y)
    density = jnp.sum(read, 0)
    velocity = moments(read) / density
    cube_side = 2 * RADIUS + 1
    step_x = bead_cell // (cube_side * cube_side) - RADIUS
    step_y = bead_cell // cube_side % cube_side - RADIUS
    step_z = bead_cell % cube_side - RADIUS
    lever = jnp.stack(
        [
            step_x.astype(jnp.float32) + bead_frac[0],
            step_y.astype(jnp.float32) + bead_frac[1],
            step_z.astype(jnp.float32) + bead_frac[2],
        ]
    )
    bead_velocity = colloid_velocity[..., None] + cross_product(colloid_spin[..., None], lever)
    filled = (jnp.arange(slots)[None, None, :] < colloid_count[:, :, None]).astype(jnp.float32)
    weight = bead_weight * filled[..., None]
    reach_x = (colloid_centre[0] % width_x)[..., None] + step_x
    reach_y = (colloid_centre[1] % width_y)[..., None] + step_y
    brick_x = reach_x // width_x
    brick_y = reach_y // width_y
    local_x = reach_x - brick_x * width_x
    local_y = reach_y - brick_y * width_y
    local_z = colloid_centre[2][..., None] + step_z
    node_code = (
        (((brick_x + 1) * 3 + brick_y + 1) * width_x + local_x) * width_y + local_y
    ) * depth + local_z
    packet = jnp.stack(
        [
            bead_velocity[0],
            bead_velocity[1],
            bead_velocity[2],
            lever[0],
            lever[1],
            lever[2],
            weight,
            node_code.astype(jnp.float32),
        ],
        0,
    )
    received = padded(packet, (("gx", 1), ("gy", 2)), 1)
    code_back = received[7].astype(jnp.int32)
    node_z = code_back % depth
    remainder = code_back // depth
    node_y = remainder % width_y
    remainder = remainder // width_y
    node_x = remainder % width_x
    direction = remainder // width_x
    place_x = jnp.arange(3)[:, None, None, None]
    place_y = jnp.arange(3)[None, :, None, None]
    accept = ((direction // 3 == 2 - place_x) & (direction % 3 == 2 - place_y)).astype(jnp.float32)
    node_index = (node_x * width_y + node_y) * depth + node_z
    sampled = velocity.reshape(3, -1)[:, node_index]
    bead_force = friction * (received[6] * accept) * (received[0:3] - sampled)
    node_force = (
        jnp.zeros((3, width_x * width_y * depth), jnp.float32)
        .at[:, node_index.reshape(-1)]
        .add(bead_force.reshape(3, -1))
    )
    node_force = node_force.reshape(3, width_x, width_y, depth)
    partial_value = jnp.concatenate(
        [jnp.sum(bead_force, -1), jnp.sum(cross_product(received[3:6], bead_force), -1)], 0
    )
    returned = padded(partial_value, (("gx", 1), ("gy", 2)), 1)
    colloid_kick = -jnp.sum(returned[:, 0::2, 0::2], (1, 2)) / BEADS
    colloid_kick = colloid_kick.reshape(6, 1, 1, slots)
    force = charge[None] * electric_field(wide_potential) + node_force
    populations_next = collide(read, density, velocity, force, flag_bit(node_flags, 6))
    return (populations_next, jnp.stack(new_ions), potential_now, colloid_kick)


def solution(mesh):
    in_specs = (
        P(None, "gx", "gy", None),
        P(None, "gx", "gy", None),
        P("gx", "gy", None),
        P("gx", "gy", None),
        P("gx", "gy"),
        P(None, "gx", "gy", None),
        P(None, "gx", "gy", None),
        P(None, "gx", "gy", None),
        P("gx", "gy", None, None),
        P(None, "gx", "gy", None, None),
        P("gx", "gy", None, None),
    )
    out_specs = (
        P(None, "gx", "gy", None),
        P(None, "gx", "gy", None),
        P("gx", "gy", None),
        P(None, "gx", "gy", None),
    )
    return jax.shard_map(local, mesh=mesh, in_specs=in_specs, out_specs=out_specs, check_vma=False)
```

profile of v0, /device:TPU:0, one launch (start us, length us, event | category | flops | bytes accessed | tf_op | source)
XLA Modules:
  0.0 502.7 jit_solution(11608313685126842506)
XLA Ops:
  10.0 5.0 %collective-permute-start.17 = (f32[8,1,1,2,2562]{4,3,2,1,0:T(2,128)S(1)}, f32[8,1,1,2,2562]{4,3,2,1,0:T(2,128)S(1)}, u32[]{:S(2)}, u32[]{:S(2)}) collective-permute-start(f32[8,1,1,2,2562]{4,3,2,1,0:T(2,128)S(1)} %constant_dynamic-update-slice_fusion.26), channel_id=1, source_target_pairs={{2,0},{4,2},{6,4},{8,6},{10,8},{12,10},{14,12},{16,14},{18,16},{20... | collective-permute-start | bytes 491912 | tf_op jit(solution)/shard_map/ppermute | solution.py:54
  15.1 1.7 fusion.177
  16.8 4.4 collective-permute-start.1
  34.5 1.6 reduce_sum.586
  37.4 1.6 reduce_sum.587
  48.9 4.4 collective-permute-start.5
  53.3 1.9 collective-permute-start.2
  55.2 1.7 collective-permute-start.3
  63.2 2.3 collective-permute-start.8
  66.9 4.4 collective-permute-done.9
  105.6 5.7 %copy.130 = f32[3,16384]{0,1:T(8,128)} copy(f32[3,16384]{1,0:T(4,128)} %maximum_divide_fusion) | data formatting | bytes 393216 | tf_op jit(solution)/shard_map/div | solution.py:228
  111.3 1.9 gather_fusion
  119.5 3.1 multiply_bitcast_fusion
  122.6 1.8 compare_select_fusion.1
  125.6 88.7 %gather_fusion.13 = f32[46116,3]{1,0:T(8,128)} fusion(f32[3,16384]{0,1:T(8,128)} %copy.130, s32[47104]{0:T(1024)S(1)} %pad_clamp_fusion), kind=kCustom, calls=%fused_computation.13 | custom fusion | bytes 1291248 | tf_op jit(solution)/shard_map/gather | solution.py:278
  214.4 13.7 %copy.131 = f32[46116,3]{0,1:T(4,128)} copy(f32[46116,3]{1,0:T(8,128)} %gather_fusion.13) | data formatting | bytes 1106784 | tf_op jit(solution)/shard_map/gather | solution.py:278
  228.0 2.8 reshape.1060
  230.8 1.7 pad_maximum_fusion
  233.1 1.7 reshape.1064
  237.9 4.4 collective-permute-start.21
  242.3 11.9 %copy.132 = f32[3,46116]{0,1:T(8,128)} copy(f32[3,46116]{1,0:T(4,128)S(1)} %copy-done.8) | data formatting | bytes 1106784 | tf_op jit(solution)/shard_map/reshape | solution.py:283
  254.2 3.8 fusion.14
  258.0 229.5 %scatter_custom_fusion = f32[3,16384]{0,1:T(8,128)} fusion(s32[46116]{0:T(1024)S(1)} %fusion.14, f32[3,46116]{0,1:T(8,128)} %copy.132, f32[]{:T(128)} %constant.324.clone.1), kind=kCustom, calls=%fused_computation.15 | custom fusion | flops 138348 | bytes 750004 | tf_op jit(solution)/shard_map/scatter-add | solution.py:283
  487.6 5.3 %copy.133 = f32[3,8,16,128]{3,2,1,0:T(8,128)S(1)} copy(f32[3,8,16,128]{0,3,2,1:T(8,128)} %bitcast.245) | data formatting | bytes 393216 | tf_op jit(solution)/shard_map/reshape | solution.py:285
  (368 shorter events, 94.7 us)
Async XLA Ops:
  9.5 48.0 %collective-permute-start.16 = (f32[8,1,1,2,2562]{4,3,2,1,0:T(2,128)S(1)}, f32[8,1,1,2,2562]{4,3,2,1,0:T(2,128)S(1)}, u32[]{:S(2)}, u32[]{:S(2)}) collective-permute-start(f32[8,1,1,2,2562]{4,3,2,1,0:T(2,128)S(1)} %constant_dynamic-update-slice_fusion.26), channel_id=1, source_target_pairs={{0,2},{2,4},{4,6},{6,8},{8,10},{10,12},{12,14},{14,16},{16,18},{18... | collective-permute-start | bytes 491912 | tf_op jit(solution)/shard_map/ppermute | solution.py:51
  10.0 49.0 %collective-permute-start.17 = (f32[8,1,1,2,2562]{4,3,2,1,0:T(2,128)S(1)}, f32[8,1,1,2,2562]{4,3,2,1,0:T(2,128)S(1)}, u32[]{:S(2)}, u32[]{:S(2)}) collective-permute-start(f32[8,1,1,2,2562]{4,3,2,1,0:T(2,128)S(1)} %constant_dynamic-update-slice_fusion.26), channel_id=1, source_target_pairs={{2,0},{4,2},{6,4},{8,6},{10,8},{12,10},{14,12},{16,14},{18,16},{20... | collective-permute-start | bytes 491912 | tf_op jit(solution)/shard_map/ppermute | solution.py:54
  16.8 26.4 %collective-permute-start = (f32[19,1,16,128]{3,2,1,0:T(8,128)}, f32[19,1,16,128]{3,2,1,0:T(8,128)}, u32[]{:S(2)}, u32[]{:S(2)}) collective-permute-start(f32[19,1,16,128]{3,2,1,0:T(8,128)} %get-tuple-element.57), channel_id=1, source_target_pairs={{0,2},{2,4},{4,6},{6,8},{8,10},{10,12},{12,14},{14,16},{16,18},{18... | collective-permute-start | bytes 466952 | tf_op jit(solution)/shard_map/ppermute | solution.py:51
  16.8 27.7 %collective-permute-start.1 = (f32[19,1,16,128]{3,2,1,0:T(8,128)}, f32[19,1,16,128]{3,2,1,0:T(8,128)}, u32[]{:S(2)}, u32[]{:S(2)}) collective-permute-start(f32[19,1,16,128]{3,2,1,0:T(8,128)} %get-tuple-element.56), channel_id=1, source_target_pairs={{2,0},{4,2},{6,4},{8,6},{10,8},{12,10},{14,12},{16,14},{18,16},{20... | collective-permute-start | bytes 466952 | tf_op jit(solution)/shard_map/ppermute | solution.py:54
  48.8 6.5 %collective-permute-start.4 = (f32[6,1,16,128]{3,2,1,0:T(8,128)S(1)}, f32[6,1,16,128]{3,2,1,0:T(8,128)S(1)}, u32[]{:S(2)}, u32[]{:S(2)}) collective-permute-start(f32[6,1,16,128]{3,2,1,0:T(8,128)S(1)} %get-tuple-element.69), channel_id=1, source_target_pairs={{0,2},{2,4},{4,6},{6,8},{8,10},{10,12},{12,14},{14,16},{16,18},{18... | collective-permute-start | bytes 147464 | tf_op jit(solution)/shard_map/ppermute | solution.py:51
  48.9 8.1 %collective-permute-start.5 = (f32[6,1,16,128]{3,2,1,0:T(8,128)S(1)}, f32[6,1,16,128]{3,2,1,0:T(8,128)S(1)}, u32[]{:S(2)}, u32[]{:S(2)}) collective-permute-start(f32[6,1,16,128]{3,2,1,0:T(8,128)S(1)} %get-tuple-element.70), channel_id=1, source_target_pairs={{2,0},{4,2},{6,4},{8,6},{10,8},{12,10},{14,12},{16,14},{18,16},{20... | collective-permute-start | bytes 147464 | tf_op jit(solution)/shard_map/ppermute | solution.py:54
  53.3 25.8 %collective-permute-start.2 = (f32[19,10,1,128]{3,2,1,0:T(1,128)S(1)}, f32[19,10,1,128]{3,2,1,0:T(1,128)S(1)}, u32[]{:S(2)}, u32[]{:S(2)}) collective-permute-start(f32[19,10,1,128]{3,2,1,0:T(1,128)S(1)} %get-tuple-element.41), channel_id=1, source_target_pairs={{0,1},{1,0},{2,3},{3,2},{4,5},{5,4},{6,7},{7,6},{8,9},{9,8},{10,11... | collective-permute-start | bytes 291848 | tf_op jit(solution)/shard_map/ppermute | solution.py:51
  55.2 24.3 %collective-permute-start.3 = (f32[19,10,1,128]{3,2,1,0:T(1,128)S(1)}, f32[19,10,1,128]{3,2,1,0:T(1,128)S(1)}, u32[]{:S(2)}, u32[]{:S(2)}) collective-permute-start(f32[19,10,1,128]{3,2,1,0:T(1,128)S(1)} %get-tuple-element.42), channel_id=1, source_target_pairs={{1,0},{0,1},{3,2},{2,3},{5,4},{4,5},{7,6},{6,7},{9,8},{8,9},{11,10... | collective-permute-start | bytes 291848 | tf_op jit(solution)/shard_map/ppermute | solution.py:54
  57.0 4.6 collective-permute-start.6
  57.5 4.8 collective-permute-start.7
  60.8 58.7 %collective-permute-start.18 = (f32[8,3,1,2,2562]{4,3,2,1,0:T(2,128)}, f32[8,3,1,2,2562]{4,3,2,1,0:T(2,128)S(1)}, u32[]{:S(2)}, u32[]{:S(2)}) collective-permute-start(f32[8,3,1,2,2562]{4,3,2,1,0:T(2,128)} %pad_maximum_fusion.2), channel_id=1, source_target_pairs={{0,1},{1,0},{2,3},{3,2},{4,5},{5,4},{6,7},{7,6},{8,9},{9,8},{10,11... | collective-permute-start | bytes 1475720 | tf_op jit(solution)/shard_map/ppermute | solution.py:51
  63.2 3.7 collective-permute-start.8
  65.5 5.8 %collective-permute-start.9 = (f32[1,16,128]{2,1,0:T(8,128)S(1)}, f32[1,16,128]{2,1,0:T(8,128)S(1)}, u32[]{:S(2)}, u32[]{:S(2)}) collective-permute-start(f32[1,16,128]{2,1,0:T(8,128)S(1)} %get-tuple-element.133), channel_id=1, source_target_pairs={{0,2},{2,4},{4,6},{6,8},{8,10},{10,12},{12,14},{14,16},{16,18},{18... | collective-permute-start | bytes 24584 | tf_op jit(solution)/shard_map/ppermute | solution.py:51
  71.3 3.7 collective-permute-start.10
  72.3 3.7 collective-permute-start.11
  75.1 44.4 %collective-permute-start.19 = (f32[8,3,1,2,2562]{4,3,2,1,0:T(2,128)}, f32[8,3,1,2,2562]{4,3,2,1,0:T(2,128)}, u32[]{:S(2)}, u32[]{:S(2)}) collective-permute-start(f32[8,3,1,2,2562]{4,3,2,1,0:T(2,128)} %pad_maximum_fusion.2), channel_id=1, source_target_pairs={{1,0},{0,1},{3,2},{2,3},{5,4},{4,5},{7,6},{6,7},{9,8},{8,9},{11,10... | collective-permute-start | bytes 1475720 | tf_op jit(solution)/shard_map/ppermute | solution.py:54
  76.8 36.4 %collective-permute-start.12 = (f32[1,16,128]{2,1,0:T(8,128)}, f32[1,16,128]{2,1,0:T(8,128)S(1)}, u32[]{:S(2)}, u32[]{:S(2)}) collective-permute-start(f32[1,16,128]{2,1,0:T(8,128)} %get-tuple-element.132), channel_id=1, source_target_pairs={{2,0},{4,2},{6,4},{8,6},{10,8},{12,10},{14,12},{16,14},{18,16},{20... | collective-permute-start | bytes 24584 | tf_op jit(solution)/shard_map/ppermute | solution.py:54
  79.1 34.2 %collective-permute-start.13 = (f32[1,16,128]{2,1,0:T(8,128)}, f32[1,16,128]{2,1,0:T(8,128)S(1)}, u32[]{:S(2)}, u32[]{:S(2)}) collective-permute-start(f32[1,16,128]{2,1,0:T(8,128)} %get-tuple-element.131), channel_id=1, source_target_pairs={{0,2},{2,4},{4,6},{6,8},{8,10},{10,12},{12,14},{14,16},{16,18},{18... | collective-permute-start | bytes 24584 | tf_op jit(solution)/shard_map/ppermute | solution.py:51
  113.3 5.0 collective-permute-start.14
  114.4 3.9 collective-permute-start.15
  237.9 259.3 %collective-permute-start.20 = (f32[6,1,3,2]{0,3,2,1:T(2,128)S(1)}, f32[6,1,3,2]{0,3,2,1:T(2,128)S(1)}, u32[]{:S(2)}, u32[]{:S(2)}) collective-permute-start(f32[6,1,3,2]{0,3,2,1:T(2,128)S(1)} %get-tuple-element.137), channel_id=1, source_target_pairs={{0,2},{2,4},{4,6},{6,8},{8,10},{10,12},{12,14},{14,16},{16,18},{18... | collective-permute-start | bytes 440 | tf_op jit(solution)/shard_map/ppermute | solution.py:51
  237.9 259.3 %collective-permute-start.21 = (f32[6,1,3,2]{0,3,2,1:T(2,128)S(1)}, f32[6,1,3,2]{0,3,2,1:T(2,128)S(1)}, u32[]{:S(2)}, u32[]{:S(2)}) collective-permute-start(f32[6,1,3,2]{0,3,2,1:T(2,128)S(1)} %get-tuple-element.138), channel_id=1, source_target_pairs={{2,0},{4,2},{6,4},{8,6},{10,8},{12,10},{14,12},{16,14},{18,16},{20... | collective-permute-start | bytes 440 | tf_op jit(solution)/shard_map/ppermute | solution.py:54
  497.3 3.6 collective-permute-start.22
  498.4 3.6 collective-permute-start.23
  (85 other events, 452.0 us)
where the time goes:
time: 505 us; the launch traced here: 503 us
  other arithmetic  288 us (57%)
  local copies, waits for them, and re-layouts  169 us (33%)
  starting transfers between devices  35.3 us (7%)
  waiting for transfers between devices  8.18 us (2%)
    scatter-add x1, other arithmetic, local(): node_force = jnp.zeros((3, width_x * width_y * depth), jnp.float32).at[:,...  230 us
    gather x3, local copies, waits for them, and re-layouts, local(): sampled = velocity.reshape(3, -1)[:, node_index]  105 us
    ppermute x12, starting transfers between devices, padded(): lax.ppermute(lax.slice_in_dim(block, 0, width, axis=dim), axis, backward)  28 us
    reshape x2, local copies, waits for them, and re-layouts, local(): bead_force.reshape(3, -1)  13.6 us
  transfers between devices with their start and end apart: 24, of which 7 were waited for; matrix products, arithmetic and copies ran while one was open for 65% of the time, Pallas kernels for 0%

commit v1 on v0

v1 whole, which is shorter than its diff:
```python
import functools

import jax
import jax.numpy as jnp
import numpy as np
from jax import lax
from jax.experimental import pallas as pl
from jax.experimental.pallas import tpu as pltpu
from jax.sharding import PartitionSpec as P

RADIUS = 6
SIDE = 2 * RADIUS + 1
YO = 8
XO = 3
CHUNK = 384
MESH = pl.DeviceIdType.MESH
F32 = jnp.float32
BF16 = jnp.bfloat16

LATTICE = np.array(
    [
        [0, 0, 0],
        [1, 0, 0],
        [-1, 0, 0],
        [0, 1, 0],
        [0, -1, 0],
        [0, 0, 1],
        [0, 0, -1],
        [1, 1, 0],
        [-1, -1, 0],
        [1, -1, 0],
        [-1, 1, 0],
        [1, 0, 1],
        [-1, 0, -1],
        [1, 0, -1],
        [-1, 0, 1],
        [0, 1, 1],
        [0, -1, -1],
        [0, 1, -1],
        [0, -1, 1],
    ]
)
OPPOSITE = [0, 2, 1, 4, 3, 6, 5, 8, 7, 10, 9, 12, 11, 14, 13, 16, 15, 18, 17]
tau_relax = 0.8
kappa_charge = 0.5
friction = 4.0
diffusion = (0.12, 0.15)
valence = (1.0, -1.0)
X_DIRS = [(1, 0), (-1, 0)]
Y_DIRS = [(0, 1), (0, -1)]
C_DIRS = [(1, 1), (1, -1), (-1, 1), (-1, -1)]
DIRS = X_DIRS + Y_DIRS + C_DIRS


def lattice_weight(i):
    if i == 0:
        return 1.0 / 3.0
    if i < 7:
        return 1.0 / 18.0
    return 1.0 / 36.0


def links(a, sign):
    return [i for i in range(19) if LATTICE[i][a] == sign]


def corner_link(sx, sy):
    return [i for i in range(19) if tuple(LATTICE[i]) == (sx, sy, 0)][0]


def total_of(terms):
    terms = list(terms)
    while len(terms) > 1:
        terms = [
            terms[j] + terms[j + 1] if j + 1 < len(terms) else terms[j]
            for j in range(0, len(terms), 2)
        ]
    return terms[0]


def momentum(pops, a):
    return total_of(pops[i] for i in links(a, 1)) - total_of(pops[i] for i in links(a, -1))


def layer(s, depth, width):
    return width - 1 - depth if s > 0 else depth


def halo(s, depth, width):
    return -1 - depth if s > 0 else width + depth


def split3(v):
    hi = v.astype(BF16)
    rest = v - hi.astype(F32)
    mid = rest.astype(BF16)
    low = (rest - mid.astype(F32)).astype(BF16)
    return hi, mid, low


def dot_t(a, b):
    return lax.dot_general(a, b, (((1,), (1,)), ((), ())), preferred_element_type=F32)


def bead_span_x(sx, width):
    if sx > 0:
        return RADIUS + width, RADIUS, 0
    if sx < 0:
        return 0, RADIUS, width - RADIUS
    return RADIUS, width, 0


def bead_span_y(sy, width):
    if sy > 0:
        return YO + width, 8, 0
    if sy < 0:
        return 0, 8, width - 8
    return YO, width, 0


def pack_kernel(
    count_ref, centre_ref, vel_ref, spin_ref, cell_ref, frac_ref, weight_ref, pops_ref, ions_ref,
    phi_ref, xs_ref, ys_ref, cs_ref, own_ref, drift_ref, base_ref,
    beads, codes, acc, field,
):
    wx, wy, depth = phi_ref.shape
    nb = cell_ref.shape[3]
    kp = beads.shape[2]
    tall = 2 * YO + wy
    planes = wx + 2 * RADIUS

    def drift_plane(x, carry):
        pops = [pops_ref[i, x] for i in range(19)]
        inv = 1.0 / total_of(pops)
        for a in range(3):
            drift_ref[a, x] = momentum(pops, a) * inv
        return carry

    lax.fori_loop(0, wx, drift_plane, 0)

    beads[...] = jnp.zeros_like(beads)
    beads[0, :, :nb] = cell_ref[0, 0].astype(F32)
    for k in range(3):
        beads[1 + k, :, :nb] = frac_ref[k, 0, 0]
    beads[4, :, :nb] = weight_ref[0, 0]
    first = lax.broadcasted_iota(jnp.int32, (2, kp), 0) == 0
    count = count_ref[0, 0]

    def pick(ref, k):
        return jnp.where(first, ref[k, 0, 0, 0], ref[k, 0, 0, 1])

    cell = beads[0]
    ix = jnp.floor((cell + 0.5) * (1.0 / (SIDE * SIDE)))
    rest = cell - ix * (SIDE * SIDE)
    iy = jnp.floor((rest + 0.5) * (1.0 / SIDE))
    iz = rest - iy * SIDE
    slot = jnp.where(first, 0, 1)
    weight = jnp.where(slot < count, beads[4], 0.0)
    lever = [idx - RADIUS + beads[1 + k] for k, idx in enumerate((ix, iy, iz))]
    vel = [pick(vel_ref, k) for k in range(3)]
    spin = [pick(spin_ref, k) for k in range(3)]
    cross = lambda p, q: [p[1] * q[2] - p[2] * q[1], p[2] * q[0] - p[0] * q[2], p[0] * q[1] - p[1] * q[0]]
    turn = cross(spin, lever)
    push = [weight * (vel[k] + turn[k]) for k in range(3)]
    twist = cross(lever, push)
    for k, v in enumerate(push + twist):
        base_ref[k] = jnp.broadcast_to(jnp.sum(v, axis=1, keepdims=True), (2, 128))
    local_x = [lax.rem(centre_ref[0, 0, 0, s], wx).astype(F32) for s in range(2)]
    local_y = [lax.rem(centre_ref[1, 0, 0, s], wy).astype(F32) for s in range(2)]
    px = ix + jnp.where(first, local_x[0], local_x[1])
    py = iy + jnp.where(first, local_y[0], local_y[1]) + (YO - RADIUS)
    codes[0] = px * tall + py
    codes[1] = iz
    codes[2] = weight
    for k in range(3):
        codes[3 + k] = weight * lever[k]
    for s in range(2):
        acc[...] = jnp.zeros_like(acc)

        def step(c, carry):
            lanes = pl.ds(pl.multiple_of(c * CHUNK, CHUNK), CHUNK)
            code = codes[0, s : s + 1, lanes].astype(jnp.int32)
            node = lax.broadcasted_iota(jnp.int32, (planes * tall, CHUNK), 0)
            place = jnp.where(node == code, 1.0, 0.0).astype(BF16)
            level = codes[1, s : s + 1, lanes].astype(jnp.int32)
            at_level = lax.broadcasted_iota(jnp.int32, (16, CHUNK), 0) == level
            values = jnp.concatenate(
                [jnp.where(at_level, codes[2 + q, s : s + 1, lanes], 0.0) for q in range(4)], 0
            )
            parts = jnp.concatenate(split3(values), 0)
            acc[...] += dot_t(place, parts)
            return carry

        lax.fori_loop(0, kp // CHUNK, step, 0)
        field[:, 64 * s : 64 * s + 64] = acc[:, 0:64] + acc[:, 64:128] + acc[:, 128:192]

    lane = lax.broadcasted_iota(jnp.int32, (1, 128), 1)
    lane_slot = lane // 64
    channel = (lane // 16) % 4
    by_slot = lambda ref, k: jnp.where(lane_slot == 0, ref[k, 0, 0, 0], ref[k, 0, 0, 1])
    v = [by_slot(vel_ref, k) for k in range(3)]
    w = [by_slot(spin_ref, k) for k in range(3)]
    zero = jnp.zeros((1, 128), F32)

    def four(*rows):
        out = zero
        for q, row in enumerate(rows):
            out = jnp.where(channel == q, row, out)
        return out

    constants = jnp.concatenate(
        [
            four(v[0], zero, -w[2], w[1]),
            four(v[1], w[2], zero, -w[0]),
            four(v[2], -w[1], w[0], zero),
            four(zero + 1.0, zero, zero, zero),
            by_slot(centre_ref, 2).astype(F32) + (lane % 16 - RADIUS).astype(F32),
            zero,
            zero,
            zero,
        ],
        0,
    )

    def charge(x, y):
        return ions_ref[0, x, y] - ions_ref[1, x, y]

    def put_beads(ref, at, sx, sy):
        x0, nx, _ = bead_span_x(sx, wx)
        y0, ny, _ = bead_span_y(sy, wy)
        for x in range(nx):
            start = (x0 + x) * tall + y0
            ref[pl.ds(at + x * ny, ny)] = field[start : start + ny]
        return at + nx * ny

    own_ref[0:8] = constants
    put_beads(own_ref, 8, 0, 0)
    for j, (sx, _) in enumerate(X_DIRS):
        out = xs_ref.at[j]
        out[0:8] = constants
        at = put_beads(out, 8, sx, 0)
        edge = layer(sx, 0, wx)
        rows = [pops_ref[i, edge] for i in links(0, sx)]
        rows += [ions_ref[0, edge], ions_ref[1, edge], charge(layer(sx, 1, wx), slice(None))]
        rows += [phi_ref[layer(sx, l, wx)] for l in range(3)] + [drift_ref[0, edge]]
        for row in rows:
            out[at : at + wy] = row
            at += wy
    for j, (_, sy) in enumerate(Y_DIRS):
        out = ys_ref.at[j]
        out[0:8] = constants
        at = put_beads(out, 8, 0, sy)
        edge = layer(sy, 0, wy)
        rows = [pops_ref[i, :, edge] for i in links(1, sy)]
        rows += [ions_ref[0, :, edge], ions_ref[1, :, edge], charge(slice(None), layer(sy, 1, wy))]
        rows += [phi_ref[:, layer(sy, l, wy)] for l in range(3)] + [drift_ref[1, :, edge]]
        for row in rows:
            out[at : at + wx] = row
            at += wx
    for j, (sx, sy) in enumerate(C_DIRS):
        out = cs_ref.at[j]
        out[0:8] = constants
        at = put_beads(out, 8, sx, sy)
        ex, ey = layer(sx, 0, wx), layer(sy, 0, wy)
        rows = [
            pops_ref[corner_link(sx, sy), ex, ey],
            charge(ex, ey),
            phi_ref[ex, ey],
            phi_ref[layer(sx, 1, wx), ey],
            phi_ref[ex, layer(sy, 1, wy)],
        ]
        for row in rows:
            out[at] = row
            at += 1
        out[at : at + 3] = jnp.zeros((3, 128), F32)


def neighbour(shape, sx, sy):
    nx, ny = shape
    return (
        lax.rem(lax.axis_index("gx") + (sx + nx), nx),
        lax.rem(lax.axis_index("gy") + (sy + ny), ny),
    )


def meet(shape):
    barrier = pltpu.get_barrier_semaphore()
    for sx, sy in DIRS:
        pl.semaphore_signal(barrier, inc=1, device_id=neighbour(shape, sx, sy), device_id_type=MESH)
    pl.semaphore_wait(barrier, len(DIRS))


def exchange_kernel(shape, xs, ys, cs, rx, ry, rc, send, recv):
    meet(shape)
    copies = []
    sources = [xs.at[0], xs.at[1], ys.at[0], ys.at[1]] + [cs.at[j] for j in range(4)]
    targets = [rx.at[0], rx.at[1], ry.at[0], ry.at[1]] + [rc.at[j] for j in range(4)]
    for d in range(8):
        copies.append(
            pltpu.make_async_remote_copy(
                src_ref=sources[d], dst_ref=targets[d], send_sem=send.at[d], recv_sem=recv.at[d],
                device_id=neighbour(shape, *DIRS[d]), device_id_type=MESH,
            )
        )
    for copy in copies:
        copy.start()
    for copy in copies:
        copy.wait()


def return_kernel(shape, beads, part_ref, base_ref, kick_ref, got, send, recv):
    meet(shape)
    copies = []
    for d, (sx, sy) in enumerate(DIRS):
        copies.append(
            pltpu.make_async_remote_copy(
                src_ref=part_ref.at[d + 1], dst_ref=got.at[d], send_sem=send.at[d],
                recv_sem=recv.at[d], device_id=neighbour(shape, -sx, -sy), device_id_type=MESH,
            )
        )
    for copy in copies:
        copy.start()
    for copy in copies:
        copy.wait()
    whole = total_of([part_ref[0]] + [got[d] for d in range(8)])
    lane = lax.broadcasted_iota(jnp.int32, (8, 128), 1)
    group = lane // 16
    for s in range(2):
        m = [
            jnp.sum(jnp.where(group == 4 * s + q, whole, 0.0), axis=1, keepdims=True)
            for q in range(4)
        ]
        mean = [m[0][k : k + 1] for k in range(3)]
        lev = [[m[1 + a][k : k + 1] for k in range(3)] for a in range(3)]
        turned = [lev[1][2] - lev[2][1], lev[2][0] - lev[0][2], lev[0][1] - lev[1][0]]
        for k, v in enumerate(mean + turned):
            value = (base_ref[k, s : s + 1] - v) * (-friction / beads)
            kick_ref[k, s : s + 1] = value


def main_kernel(
    pops_ref, ions_ref, phi_ref, flags_ref, drift_ref, own_ref, rx, ry, rc,
    pops_out, ions_out, phi_out, part_ref,
    ext, eion, echarge, edrift, ephi, ephi1, ephi2, held, marks, bead_rows, pushes, vels,
):
    wx, wy, depth = phi_ref.shape
    inner = slice(YO, YO + wy)
    lanes = lax.broadcasted_iota(jnp.int32, (1, depth), 1)

    for i in range(19):
        ext[i, 1 : 1 + wx, inner] = pops_ref[i]
    for s in range(2):
        eion[s, 1 : 1 + wx, inner] = ions_ref[s]
    echarge[XO : XO + wx, inner] = ions_ref[0] - ions_ref[1]
    ephi[XO : XO + wx, inner] = phi_ref[...]
    for a in range(2):
        edrift[a, 1 : 1 + wx, inner] = drift_ref[a]
    held[...] = jnp.zeros_like(held)

    def take_beads(ref, n, sx, sy):
        _, nx, tx = bead_span_x(sx, wx)
        _, ny, ty = bead_span_y(sy, wy)
        marks[n] = ref[0:8]
        for x in range(nx):
            held[n, tx + x, ty : ty + ny] = ref[8 + x * ny : 8 + (x + 1) * ny]
        return 8 + nx * ny

    take_beads(own_ref, 0, 0, 0)
    for j, (sx, _) in enumerate(X_DIRS):
        src = rx.at[j]
        at = take_beads(src, 1 + j, sx, 0)
        edge = 1 + halo(sx, 0, wx)
        for i in links(0, sx):
            ext[i, edge, inner] = src[at : at + wy]
            at += wy
        for s in range(2):
            eion[s, edge, inner] = src[at : at + wy]
            at += wy
        echarge[XO + halo(sx, 0, wx), inner] = eion[0, edge, inner] - eion[1, edge, inner]
        echarge[XO + halo(sx, 1, wx), inner] = src[at : at + wy]
        at += wy
        for l in range(3):
            ephi[XO + halo(sx, l, wx), inner] = src[at : at + wy]
            at += wy
        edrift[0, edge, inner] = src[at : at + wy]
    for j, (_, sy) in enumerate(Y_DIRS):
        src = ry.at[j]
        at = take_beads(src, 3 + j, 0, sy)
        edge = YO + halo(sy, 0, wy)
        for i in links(1, sy):
            ext[i, 1 : 1 + wx, edge] = src[at : at + wx]
            at += wx
        ion0, ion1 = src[at : at + wx], src[at + wx : at + 2 * wx]
        eion[0, 1 : 1 + wx, edge] = ion0
        eion[1, 1 : 1 + wx, edge] = ion1
        at += 2 * wx
        echarge[XO : XO + wx, edge] = ion0 - ion1
        echarge[XO : XO + wx, YO + halo(sy, 1, wy)] = src[at : at + wx]
        at += wx
        for l in range(3):
            ephi[XO : XO + wx, YO + halo(sy, l, wy)] = src[at : at + wx]
            at += wx
        edrift[1, 1 : 1 + wx, edge] = src[at : at + wx]
    for j, (sx, sy) in enumerate(C_DIRS):
        src = rc.at[j]
        at = take_beads(src, 5 + j, sx, sy)
        hx, hy = halo(sx, 0, wx), YO + halo(sy, 0, wy)
        ext[corner_link(sx, sy), 1 + hx, hy] = src[at]
        echarge[XO + hx, hy] = src[at + 1]
        ephi[XO + hx, hy] = src[at + 2]
        ephi[XO + halo(sx, 1, wx), hy] = src[at + 3]
        ephi[XO + hx, YO + halo(sy, 1, wy)] = src[at + 4]

    def up(v):
        return jnp.where(lanes == depth - 1, 0.0, pltpu.roll(v, depth - 1, v.ndim - 1))

    def down(v):
        return jnp.where(lanes == 0, 0.0, pltpu.roll(v, 1, v.ndim - 1))

    def sweep(old, new, rim):
        lo, n = YO - rim, wy + 2 * rim

        def plane(t, carry):
            x = XO - rim + t
            mid = old[x, lo : lo + n]
            around = old[x + 1, lo : lo + n] + old[x - 1, lo : lo + n]
            around = around + (old[x, lo + 1 : lo + n + 1] + old[x, lo - 1 : lo + n - 1])
            around = around + (up(mid) + down(mid))
            new[x, lo : lo + n] = (around + kappa_charge * echarge[x, lo : lo + n]) / 6.0
            return carry

        lax.fori_loop(0, wx + 2 * rim, plane, 0)

    sweep(ephi, ephi1, 2)
    sweep(ephi1, ephi2, 1)

    reach = []
    for n in range(9):
        z = marks[n, 4:5].astype(jnp.int32)
        level = lax.broadcasted_iota(jnp.int32, (depth, 128), 0)
        reach.append(jnp.where(level == z, 1.0, 0.0).astype(BF16))
    rows = wx * wy
    for n in range(9):
        block = held[n].reshape(rows, 128)
        for k in range(4):
            hi, mid, low = split3(block * marks[n, k : k + 1])
            bead_rows[0, k * rows : (k + 1) * rows, n * 128 : (n + 1) * 128] = hi
            bead_rows[1, k * rows : (k + 1) * rows, n * 128 : (n + 1) * 128] = mid
            bead_rows[2, k * rows : (k + 1) * rows, n * 128 : (n + 1) * 128] = low
    everywhere = jnp.concatenate(reach, 1)
    spread = total_of([dot_t(bead_rows[p], everywhere) for p in range(3)])
    pushes[...] = spread.reshape(4, wx, wy, depth)

    def node_plane(x, carry):
        flags = flags_ref[x]
        bit = lambda b: ((flags >> b) & 1).astype(F32)
        opened = [bit(b) for b in range(6)]
        solid = bit(6) > 0.5
        phi = ephi2[XO + x, inner]
        phi_out[x] = phi
        phi_low = [ephi2[XO + x - 1, inner], ephi2[XO + x, YO - 1 : YO - 1 + wy]]
        phi_high = [ephi2[XO + x + 1, inner], ephi2[XO + x, YO + 1 : YO + 1 + wy]]
        phi_z_low, phi_z_high = pltpu.roll(phi, 1, 1), pltpu.roll(phi, depth - 1, 1)
        drift = [drift_ref[a, x] for a in range(3)]
        drift_low = [edrift[0, x, inner], edrift[1, 1 + x, YO - 1 : YO - 1 + wy]]
        drift_high = [edrift[0, x + 2, inner], edrift[1, 1 + x, YO + 1 : YO + 1 + wy]]
        drift_z_low = pltpu.roll(drift[2], 1, 1)

        def flux(lo_ion, hi_ion, lo_phi, hi_phi, lo_drift, hi_drift, gate, s):
            middle = 0.5 * (lo_ion + hi_ion)
            diffusive = -diffusion[s] * (
                (hi_ion - lo_ion) + valence[s] * middle * (hi_phi - lo_phi)
            )
            return gate * (diffusive + 0.5 * (lo_drift + hi_drift) * middle)

        both = []
        for s in range(2):
            ion = eion[s, 1 + x, inner]
            both.append(ion)
            ion_low = [eion[s, x, inner], eion[s, 1 + x, YO - 1 : YO - 1 + wy]]
            ion_high = [eion[s, x + 2, inner], eion[s, 1 + x, YO + 1 : YO + 1 + wy]]
            divergence = 0.0
            for a in range(2):
                entering = flux(
                    ion_low[a], ion, phi_low[a], phi, drift_low[a], drift[a], opened[2 * a], s
                )
                leaving = flux(
                    ion, ion_high[a], phi, phi_high[a], drift[a], drift_high[a], opened[2 * a + 1], s
                )
                divergence = divergence + (leaving - entering)
            entering = flux(
                pltpu.roll(ion, 1, 1), ion, phi_z_low, phi, drift_z_low, drift[2], opened[4], s
            )
            divergence = divergence + (pltpu.roll(entering, depth - 1, 1) - entering)
            ions_out[s, x] = ion - divergence
        charge = both[0] - both[1]

        read = []
        for i in range(19):
            sx, sy, sz = (int(c) for c in LATTICE[i])
            v = ext[i, 1 + x - sx, YO - sy : YO - sy + wy]
            read.append(v if sz == 0 else pltpu.roll(v, sz % depth, 1))
        density = total_of(read)
        inverse = 1.0 / density
        field = [
            (phi_low[0] - phi_high[0]) * 0.5,
            (phi_low[1] - phi_high[1]) * 0.5,
            (jnp.where(lanes == 0, 0.0, phi_z_low) - jnp.where(lanes == depth - 1, 0.0, phi_z_high))
            * 0.5,
        ]
        shifted = []
        for a in range(3):
            velocity = momentum(read, a) * inverse
            vels[a, x] = velocity
            force = charge * field[a] + friction * (pushes[a, x] - pushes[3, x] * velocity)
            shifted.append(velocity + tau_relax * force * inverse)
        base = 1.0 - 1.5 * (
            shifted[0] * shifted[0] + shifted[1] * shifted[1] + shifted[2] * shifted[2]
        )
        scaled = [w * density * (1.0 / tau_relax) for w in (1.0 / 3.0, 1.0 / 18.0, 1.0 / 36.0)]
        keep = 1.0 - 1.0 / tau_relax
        pops_out[0, x] = jnp.where(solid, read[0], keep * read[0] + scaled[0] * base)
        for i in range(1, 19, 2):
            along = 0.0
            for a in range(3):
                if LATTICE[i][a] != 0:
                    along = along + float(LATTICE[i][a]) * shifted[a]
            even = base + 4.5 * along * along
            odd = 3.0 * along
            scale = scaled[1] if i < 7 else scaled[2]
            pops_out[i, x] = jnp.where(
                solid, read[i + 1], keep * read[i] + scale * (even + odd)
            )
            pops_out[i + 1, x] = jnp.where(
                solid, read[i], keep * read[i + 1] + scale * (even - odd)
            )
        return carry

    lax.fori_loop(0, wx, node_plane, 0)

    parts = split3(vels[...].reshape(3 * rows, depth))
    for n in range(9):
        sampled = total_of(
            [lax.dot_general(p, reach[n], (((1,), (0,)), ((), ())), preferred_element_type=F32)
             for p in parts]
        )
        block = held[n].reshape(rows, 128)
        for k in range(3):
            part_ref[n, k : k + 1] = jnp.sum(
                block * sampled[k * rows : (k + 1) * rows], axis=0, keepdims=True
            )
        part_ref[n, 3:8] = jnp.zeros((5, 128), F32)


def local(
    shape, populations, ion_density, potential, node_flags, colloid_count, colloid_centre,
    colloid_velocity, colloid_spin, bead_cell, bead_frac, bead_weight,
):
    wx, wy, depth = potential.shape
    beads = bead_cell.shape[3]
    kp = -(-beads // CHUNK) * CHUNK
    vmem = pl.BlockSpec(memory_space=pltpu.VMEM)
    smem = pl.BlockSpec(memory_space=pltpu.SMEM)
    array = lambda *dims: jax.ShapeDtypeStruct(dims, F32)
    tall, wide = wy + 2 * YO, wx + 2
    x_rows = 8 + RADIUS * wy + 12 * wy
    y_rows = 8 + wx * 8 + 12 * wx
    c_rows = 8 + RADIUS * 8 + 8
    slabs = [array(2, x_rows, depth), array(2, y_rows, depth), array(4, c_rows, depth)]
    xs, ys, cs, own, drift, base = pl.pallas_call(
        pack_kernel,
        out_shape=slabs
        + [array(8 + wx * wy, depth), array(3, wx, wy, depth), array(6, 2, 128)],
        in_specs=[smem] * 4 + [vmem] * 6,
        out_specs=[vmem] * 6,
        scratch_shapes=[
            pltpu.VMEM((5, 2, kp), F32),
            pltpu.VMEM((6, 2, kp), F32),
            pltpu.VMEM(((wx + 2 * RADIUS) * tall, 192), F32),
            pltpu.VMEM(((wx + 2 * RADIUS) * tall, 128), F32),
        ],
    )(
        colloid_count, colloid_centre, colloid_velocity, colloid_spin, bead_cell, bead_frac,
        bead_weight, populations, ion_density, potential,
    )
    rx, ry, rc = pl.pallas_call(
        functools.partial(exchange_kernel, shape),
        out_shape=slabs,
        in_specs=[vmem] * 3,
        out_specs=[vmem] * 3,
        scratch_shapes=[pltpu.SemaphoreType.DMA((8,)), pltpu.SemaphoreType.DMA((8,))],
        compiler_params=pltpu.CompilerParams(collective_id=0, has_side_effects=True),
    )(xs, ys, cs)
    pops_next, ions_next, phi_next, parts = pl.pallas_call(
        main_kernel,
        out_shape=[
            array(*populations.shape), array(*ion_density.shape), array(*potential.shape),
            array(9, 8, 128),
        ],
        in_specs=[vmem] * 9,
        out_specs=[vmem] * 4,
        scratch_shapes=[
            pltpu.VMEM((19, wide, tall, depth), F32),
            pltpu.VMEM((2, wide, tall, depth), F32),
            pltpu.VMEM((wx + 2 * XO, tall, depth), F32),
            pltpu.VMEM((2, wide, tall, depth), F32),
            pltpu.VMEM((wx + 2 * XO, tall, depth), F32),
            pltpu.VMEM((wx + 2 * XO, tall, depth), F32),
            pltpu.VMEM((wx + 2 * XO, tall, depth), F32),
            pltpu.VMEM((9, wx, wy, 128), F32),
            pltpu.VMEM((9, 8, 128), F32),
            pltpu.VMEM((3, 4 * wx * wy, 9 * 128), BF16),
            pltpu.VMEM((4, wx, wy, depth), F32),
            pltpu.VMEM((3, wx, wy, depth), F32),
        ],
    )(populations, ion_density, potential, node_flags, drift, own, rx, ry, rc)
    kick = pl.pallas_call(
        functools.partial(return_kernel, shape, float(beads)),
        out_shape=array(6, 2, 128),
        in_specs=[vmem] * 2,
        out_specs=vmem,
        scratch_shapes=[
            pltpu.VMEM((8, 8, 128), F32),
            pltpu.SemaphoreType.DMA((8,)),
            pltpu.SemaphoreType.DMA((8,)),
        ],
        compiler_params=pltpu.CompilerParams(collective_id=1, has_side_effects=True),
    )(parts, base)
    return pops_next, ions_next, phi_next, kick[:, :, 0].reshape(6, 1, 1, 2)


def solution(mesh):
    in_specs = (
        P(None, "gx", "gy", None),
        P(None, "gx", "gy", None),
        P("gx", "gy", None),
        P("gx", "gy", None),
        P("gx", "gy"),
        P(None, "gx", "gy", None),
        P(None, "gx", "gy", None),
        P(None, "gx", "gy", None),
        P("gx", "gy", None, None),
        P(None, "gx", "gy", None, None),
        P("gx", "gy", None, None),
    )
    out_specs = (
        P(None, "gx", "gy", None),
        P(None, "gx", "gy", None),
        P("gx", "gy", None),
        P(None, "gx", "gy", None),
    )
    shape = (mesh.shape["gx"], mesh.shape["gy"])
    return jax.shard_map(
        functools.partial(local, shape), mesh=mesh, in_specs=in_specs, out_specs=out_specs,
        check_vma=False,
    )
```

time: 505 us -> 45.7 us (0.09)
  other arithmetic: 288 us -> 0 us
  local copies, waits for them, and re-layouts: 169 us -> 5.29 us
  Pallas kernels: 0 us -> 38.7 us
  starting transfers between devices: 35.3 us -> 0 us
  waiting for transfers between devices: 8.18 us -> 0 us
    scatter-add x1 -> x0, other arithmetic: 230 us -> none  [local(): node_force = jnp.zeros((3, width_x * width_y * depth), jnp.float32).at[:,...]
    gather x16 -> x0, local copies, waits for them, and re-layouts: 123 us -> none  [the longest x3 105 us: local(): sampled = velocity.reshape(3, -1)[:, node_index]]
    pallas_call x0 -> x4, Pallas kernels: none -> 38.7 us  [the longest x1 13.3 us: local(): pl.pallas_call(functools.partial(exchange_kernel, shape), out_shape=slabs...]
    ppermute x24 -> x0, starting transfers between devices: 35.3 us -> none  [the longest x12 28 us: padded(): lax.ppermute(lax.slice_in_dim(block, 0, width, axis=dim), axis, backward)]
    reshape x3 -> x0, local copies, waits for them, and re-layouts: 18.9 us -> none  [the longest x2 13.6 us: local(): bead_force.reshape(3, -1)]
    reduce_sum x17 -> x0, other arithmetic: 18 us -> none  [the longest x6 8.52 us: moments(): jnp.sum(pops[MINUS_SETS[a]], 0)]
    concatenate x11 -> x0, local copies, waits for them, and re-layouts: 8.28 us -> none  [the longest x10 7.16 us: stream_from(): results.append(jnp.roll(shifted_block, int(LATTICE[i][2]), 2))]
    ppermute x24 -> x0, waiting for transfers between devices: 8.18 us -> none  [the longest x12 4.99 us: padded(): lax.ppermute(lax.slice_in_dim(block, block.shape[dim] - width, None, axis...]
  transfers between devices with their start and end apart: 24 -> 0, of which waited for: 7 -> 0; matrix products, arithmetic and copies ran while one was open for 65% -> 0% of each run, Pallas kernels for 0% -> 0%
where the time goes in v1:
time: 45.7 us; the launch traced here: 45.3 us
  Pallas kernels  38.7 us (85%)
  local copies, waits for them, and re-layouts  5.29 us (12%)
  between operations  1.3 us (3%)
    pallas_call x1, Pallas kernels, local(): pl.pallas_call(functools.partial(exchange_kernel, shape), out_shape=slabs...  13.3 us
    pallas_call x1, Pallas kernels, local(): pl.pallas_call(functools.partial(return_kernel, shape, float(beads)), out...  8.74 us
    pallas_call x1, Pallas kernels, local(): pl.pallas_call(main_kernel, out_shape=[array(*populations.shape), array(*...  8.55 us
    pallas_call x1, Pallas kernels, local(): pl.pallas_call(pack_kernel, out_shape=slabs + [array(8 + wx * wy, depth),...  8.12 us
    unnamed x3, local copies, waits for them, and re-layouts  3.95 us
    slice x1, local copies, waits for them, and re-layouts, local(): return (pops_next, ions_next, phi_next, kick[:, :, 0].reshape(6, 1, 1, 2))  1.34 us

profile of v1, /device:TPU:0, one launch (start us, length us, event | category | flops | bytes accessed | tf_op | source)
XLA Modules:
  0.0 45.3 jit_solution(9829727165984274906)
XLA Ops:
  1.3 1.3 %copy.15.centre_ref = s32[3,1,1,2]{3,2,1,0:T(1,128)} copy(s32[3,1,1,2]{0,3,2,1:T(2,128)} %param.16) | data formatting | bytes 48 | tf_op args[5]
  2.6 1.3 %copy.16.vel_ref = f32[3,1,1,2]{3,2,1,0:T(1,128)} copy(f32[3,1,1,2]{0,3,2,1:T(2,128)} %param.17) | data formatting | bytes 48 | tf_op args[6]
  3.9 1.3 %copy.17.spin_ref = f32[3,1,1,2]{3,2,1,0:T(1,128)} copy(f32[3,1,1,2]{0,3,2,1:T(2,128)} %param.18) | data formatting | bytes 48 | tf_op args[7]
  5.2 8.1 %shard_map.138 = (f32[2,296,128]{2,1,0:T(8,128)}, f32[2,168,128]{2,1,0:T(8,128)}, f32[4,64,128]{2,1,0:T(8,128)}, f32[136,128]{1,0:T(8,128)}, f32[3,8,16,128]{3,2,1,0:T(8,128)}, /*index=5*/f32[6,2,128]{2,1,0:T(2,128)}) custom-call(s32[1,1]{1,0:T(1,128)S(6)} %copy.19.count_ref, s32[3,1,1,2]{3,2,1,0:T(1,128)} %copy.15.centre_ref, f32[3,1,1,2]{3,2,1,0:T(1,128)} %copy.16.vel_ref, ...), custom_call_target="tpu_custom_call" | custom-call | tf_op jit(solution)/shard_map/pallas_call | solution.py:570
  13.3 13.3 %shard_map.139 = (f32[2,296,128]{2,1,0:T(8,128)}, f32[2,168,128]{2,1,0:T(8,128)}, f32[4,64,128]{2,1,0:T(8,128)}) custom-call(f32[2,296,128]{2,1,0:T(8,128)} %get-tuple-element.19.xs, f32[2,168,128]{2,1,0:T(8,128)} %get-tuple-element.20.ys, f32[4,64,128]{2,1,0:T(8,128)} %get-tuple-element.21.cs), custom_call_target="tpu_custom_call" | custom-call | tf_op jit(solution)/shard_map/pallas_call | solution.py:586
  26.7 8.6 %shard_map.140 = (f32[19,8,16,128]{3,2,1,0:T(8,128)}, f32[2,8,16,128]{3,2,1,0:T(8,128)}, f32[8,16,128]{2,1,0:T(8,128)}, f32[9,8,128]{2,1,0:T(8,128)}) custom-call(f32[19,8,16,128]{3,2,1,0:T(8,128)} %pops_ref.3, f32[2,8,16,128]{3,2,1,0:T(8,128)} %ions_ref.3, f32[8,16,128]{2,1,0:T(8,128)} %phi_ref.3, s32[8,16,128]{2,1,0:T(8,128)} %flags_ref.1, ...), custom_call_target="tpu_custom_call" | custom-call | tf_op jit(solution)/shard_map/pallas_call | solution.py:594
  35.2 8.7 %shard_map.141 = f32[6,2,128]{2,1,0:T(2,128)} custom-call(f32[9,8,128]{2,1,0:T(8,128)} %get-tuple-element.28.part_ref, f32[6,2,128]{2,1,0:T(2,128)} %get-tuple-element.29.base_ref), custom_call_target="tpu_custom_call" | custom-call | tf_op jit(solution)/shard_map/pallas_call | solution.py:617
  44.0 1.3 %copy.18 = f32[6,2,1]{0,1,2:T(2,128)} copy(f32[6,2,1]{2,1,0:T(2,128)} %bitcast.2) | data formatting | bytes 96 | tf_op jit(solution)/shard_map/slice | solution.py:629

commit v2 on v1

v2 whole, which is shorter than its diff:
```python
import functools

import jax
import jax.numpy as jnp
import numpy as np
from jax import lax
from jax.experimental import pallas as pl
from jax.experimental.pallas import tpu as pltpu
from jax.sharding import PartitionSpec as P

RADIUS = 6
SIDE = 2 * RADIUS + 1
YO = 8
XO = 3
MESH = pl.DeviceIdType.MESH
F32 = jnp.float32
BF16 = jnp.bfloat16

LATTICE = np.array(
    [
        [0, 0, 0],
        [1, 0, 0],
        [-1, 0, 0],
        [0, 1, 0],
        [0, -1, 0],
        [0, 0, 1],
        [0, 0, -1],
        [1, 1, 0],
        [-1, -1, 0],
        [1, -1, 0],
        [-1, 1, 0],
        [1, 0, 1],
        [-1, 0, -1],
        [1, 0, -1],
        [-1, 0, 1],
        [0, 1, 1],
        [0, -1, -1],
        [0, 1, -1],
        [0, -1, 1],
    ]
)
OPPOSITE = [0, 2, 1, 4, 3, 6, 5, 8, 7, 10, 9, 12, 11, 14, 13, 16, 15, 18, 17]
tau_relax = 0.8
kappa_charge = 0.5
friction = 4.0
diffusion = (0.12, 0.15)
valence = (1.0, -1.0)
X_DIRS = [(1, 0), (-1, 0)]
Y_DIRS = [(0, 1), (0, -1)]
C_DIRS = [(1, 1), (1, -1), (-1, 1), (-1, -1)]
DIRS = X_DIRS + Y_DIRS + C_DIRS


def lattice_weight(i):
    if i == 0:
        return 1.0 / 3.0
    if i < 7:
        return 1.0 / 18.0
    return 1.0 / 36.0


def links(a, sign):
    return [i for i in range(19) if LATTICE[i][a] == sign]


def corner_link(sx, sy):
    return [i for i in range(19) if tuple(LATTICE[i]) == (sx, sy, 0)][0]


def total_of(terms):
    terms = list(terms)
    while len(terms) > 1:
        terms = [
            terms[j] + terms[j + 1] if j + 1 < len(terms) else terms[j]
            for j in range(0, len(terms), 2)
        ]
    return terms[0]


def momentum(pops, a):
    return total_of(pops[i] for i in links(a, 1)) - total_of(pops[i] for i in links(a, -1))


def layer(s, depth, width):
    return width - 1 - depth if s > 0 else depth


def halo(s, depth, width):
    return -1 - depth if s > 0 else width + depth


def split3(v):
    hi = v.astype(BF16)
    rest = v - hi.astype(F32)
    mid = rest.astype(BF16)
    low = (rest - mid.astype(F32)).astype(BF16)
    return hi, mid, low


def dot_t(a, b):
    return lax.dot_general(a, b, (((1,), (1,)), ((), ())), preferred_element_type=F32)


def bead_span_x(sx, width):
    if sx > 0:
        return RADIUS + width, RADIUS, 0
    if sx < 0:
        return 0, RADIUS, width - RADIUS
    return RADIUS, width, 0


def bead_span_y(sy, width):
    if sy > 0:
        return YO + width, 8, 0
    if sy < 0:
        return 0, 8, width - 8
    return YO, width, 0


def neighbour(shape, sx, sy):
    nx, ny = shape
    return (
        lax.rem(lax.axis_index("gx") + (sx + nx), nx),
        lax.rem(lax.axis_index("gy") + (sy + ny), ny),
    )


def send_all(shape, sources, targets, send, recv, way):
    copies = []
    for d, (sx, sy) in enumerate(DIRS):
        copies.append(
            pltpu.make_async_remote_copy(
                src_ref=sources[d], dst_ref=targets[d], send_sem=send.at[d], recv_sem=recv.at[d],
                device_id=neighbour(shape, way * sx, way * sy), device_id_type=MESH,
            )
        )
    for copy in copies:
        copy.start()
    return copies


def eight(x, y, c):
    return [x.at[0], x.at[1], y.at[0], y.at[1]] + [c.at[j] for j in range(4)]


def first_kernel(
    shape, count_ref, centre_ref, vel_ref, spin_ref, cell_ref, frac_ref, weight_ref, pops_ref,
    ions_ref, phi_ref, flags_ref,
    read_out, shifted_out, ions_out, phi_out, kick_ref,
    xs, ys, cs, rx, ry, rc, bxs, bys, bcs, bxr, byr, bcr, own,
    drift_ref, beads, codes, acc, field,
    ext, eion, echarge, edrift, ephi, ephi1, ephi2, held, marks, bead_rows, pushes, vels, dens,
    part, got, send, recv,
):
    wx, wy, depth = phi_ref.shape
    nb = cell_ref.shape[3]
    kp = beads.shape[2]
    chunk = kp // 2
    tall = 2 * YO + wy
    span_x = wx + 2 * RADIUS
    inner = slice(YO, YO + wy)
    lanes = lax.broadcasted_iota(jnp.int32, (1, depth), 1)
    rows = wx * wy

    barrier = pltpu.get_barrier_semaphore()
    for sx, sy in DIRS:
        pl.semaphore_signal(barrier, inc=1, device_id=neighbour(shape, sx, sy), device_id_type=MESH)

    def drift_plane(x, carry):
        pops = [pops_ref[i, x] for i in range(19)]
        inv = 1.0 / total_of(pops)
        for a in range(3):
            drift_ref[a, x] = momentum(pops, a) * inv
        return carry

    lax.fori_loop(0, wx, drift_plane, 0)

    def charge_at(x, y):
        return ions_ref[0, x, y] - ions_ref[1, x, y]

    for j, (sx, _) in enumerate(X_DIRS):
        out, at, edge = xs.at[j], 0, layer(sx, 0, wx)
        parts = [pops_ref[i, edge] for i in links(0, sx)]
        parts += [ions_ref[0, edge], ions_ref[1, edge], charge_at(layer(sx, 1, wx), slice(None))]
        parts += [phi_ref[layer(sx, l, wx)] for l in range(3)] + [drift_ref[0, edge]]
        for row in parts:
            out[at : at + wy] = row
            at += wy
    for j, (_, sy) in enumerate(Y_DIRS):
        out, at, edge = ys.at[j], 0, layer(sy, 0, wy)
        parts = [pops_ref[i, :, edge] for i in links(1, sy)]
        parts += [ions_ref[0, :, edge], ions_ref[1, :, edge]]
        parts += [charge_at(slice(None), layer(sy, 1, wy))]
        parts += [phi_ref[:, layer(sy, l, wy)] for l in range(3)] + [drift_ref[1, :, edge]]
        for row in parts:
            out[at : at + wx] = row
            at += wx
    for j, (sx, sy) in enumerate(C_DIRS):
        out = cs.at[j]
        ex, ey = layer(sx, 0, wx), layer(sy, 0, wy)
        parts = [
            pops_ref[corner_link(sx, sy), ex, ey],
            charge_at(ex, ey),
            phi_ref[ex, ey],
            phi_ref[layer(sx, 1, wx), ey],
            phi_ref[ex, layer(sy, 1, wy)],
        ]
        for at, row in enumerate(parts):
            out[at] = row
        out[5:8] = jnp.zeros((3, depth), F32)
    pl.semaphore_wait(barrier, len(DIRS))
    halos = send_all(
        shape, eight(xs, ys, cs), eight(rx, ry, rc), send.at[0], recv.at[0], 1
    )

    beads[...] = jnp.zeros_like(beads)
    beads[0, :, :nb] = cell_ref[0, 0].astype(F32)
    for k in range(3):
        beads[1 + k, :, :nb] = frac_ref[k, 0, 0]
    beads[4, :, :nb] = weight_ref[0, 0]
    first = lax.broadcasted_iota(jnp.int32, (2, kp), 0) == 0
    count = count_ref[0, 0]

    def pick(ref, k):
        return jnp.where(first, ref[0, k], ref[1, k])

    cell = beads[0]
    ix = jnp.floor((cell + 0.5) * (1.0 / (SIDE * SIDE)))
    rest = cell - ix * (SIDE * SIDE)
    iy = jnp.floor((rest + 0.5) * (1.0 / SIDE))
    iz = rest - iy * SIDE
    slot = jnp.where(first, 0, 1)
    weight = jnp.where(slot < count, beads[4], 0.0)
    lever = [idx - RADIUS + beads[1 + k] for k, idx in enumerate((ix, iy, iz))]
    local_y = [lax.rem(centre_ref[s, 1], wy).astype(F32) for s in range(2)]
    py = iy + jnp.where(first, local_y[0], local_y[1]) + (YO - RADIUS)
    codes[0] = ix * tall + py
    codes[1] = iz
    codes[2] = weight
    for k in range(3):
        codes[3 + k] = weight * lever[k]
    acc[0 : wx - 1] = jnp.zeros((wx - 1, tall, 192), F32)
    acc[wx - 1 + SIDE :] = jnp.zeros((wx - 1, tall, 192), F32)
    for s in range(2):

        def cells(c):
            span = pl.ds(pl.multiple_of(c * chunk, 128), chunk)
            code = codes[0, s : s + 1, span].astype(jnp.int32)
            node = lax.broadcasted_iota(jnp.int32, (SIDE * tall, chunk), 0)
            place = jnp.where(node == code, 1.0, 0.0).astype(BF16)
            level = codes[1, s : s + 1, span].astype(jnp.int32)
            at_level = lax.broadcasted_iota(jnp.int32, (16, chunk), 0) == level
            values = jnp.concatenate(
                [jnp.where(at_level, codes[2 + q, s : s + 1, span], 0.0) for q in range(4)], 0
            )
            return dot_t(place, jnp.concatenate(split3(values), 0)).reshape(SIDE, tall, 192)

        box = slice(wx - 1, wx - 1 + SIDE)
        acc[box] = cells(0)
        acc[box] += cells(1)
        offset = wx - 1 - lax.rem(centre_ref[s, 0], wx)
        for x in range(span_x):
            plane = acc[offset + x]
            field[x * tall : (x + 1) * tall, 64 * s : 64 * s + 64] = (
                plane[:, 0:64] + plane[:, 64:128] + plane[:, 128:192]
            )

    lane = lax.broadcasted_iota(jnp.int32, (1, 128), 1)
    lane_slot = lane // 64
    channel = (lane // 16) % 4
    by_slot = lambda ref, k: jnp.where(lane_slot == 0, ref[0, k], ref[1, k])
    v = [by_slot(vel_ref, k) for k in range(3)]
    w = [by_slot(spin_ref, k) for k in range(3)]
    zero = jnp.zeros((1, 128), F32)

    def four(*terms):
        out = zero
        for q, row in enumerate(terms):
            out = jnp.where(channel == q, row, out)
        return out

    constants = jnp.concatenate(
        [
            four(v[0], zero, -w[2], w[1]),
            four(v[1], w[2], zero, -w[0]),
            four(v[2], -w[1], w[0], zero),
            four(zero + 1.0, zero, zero, zero),
            by_slot(centre_ref, 2).astype(F32) + (lane % 16 - RADIUS).astype(F32),
            zero,
            zero,
            zero,
        ],
        0,
    )

    def put_beads(ref, sx, sy):
        ref[0:8] = constants
        x0, nx, _ = bead_span_x(sx, wx)
        y0, ny, _ = bead_span_y(sy, wy)
        for x in range(nx):
            start = (x0 + x) * tall + y0
            ref[8 + x * ny : 8 + (x + 1) * ny] = field[start : start + ny]

    for ref, (sx, sy) in zip(eight(bxs, bys, bcs), DIRS):
        put_beads(ref, sx, sy)
    put_beads(own, 0, 0)
    spheres = send_all(
        shape, eight(bxs, bys, bcs), eight(bxr, byr, bcr), send.at[1], recv.at[1], 1
    )

    spread_vel = [pick(vel_ref, k) for k in range(3)]
    spin = [pick(spin_ref, k) for k in range(3)]
    cross = lambda p, q: [p[1] * q[2] - p[2] * q[1], p[2] * q[0] - p[0] * q[2], p[0] * q[1] - p[1] * q[0]]
    turn = cross(spin, lever)
    push = [weight * (spread_vel[k] + turn[k]) for k in range(3)]
    twist = cross(lever, push)
    known = [jnp.sum(t, axis=1, keepdims=True) for t in push + twist]

    for i in range(19):
        ext[i, 1 : 1 + wx, inner] = pops_ref[i]
    for s in range(2):
        eion[s, 1 : 1 + wx, inner] = ions_ref[s]
    echarge[XO : XO + wx, inner] = ions_ref[0] - ions_ref[1]
    ephi[XO : XO + wx, inner] = phi_ref[...]
    for a in range(2):
        edrift[a, 1 : 1 + wx, inner] = drift_ref[a]
    held[...] = jnp.zeros_like(held)
    for copy in halos:
        copy.wait()
    for j, (sx, _) in enumerate(X_DIRS):
        src, at, edge = rx.at[j], 0, 1 + halo(sx, 0, wx)
        for i in links(0, sx):
            ext[i, edge, inner] = src[at : at + wy]
            at += wy
        for s in range(2):
            eion[s, edge, inner] = src[at : at + wy]
            at += wy
        echarge[XO + halo(sx, 0, wx), inner] = eion[0, edge, inner] - eion[1, edge, inner]
        echarge[XO + halo(sx, 1, wx), inner] = src[at : at + wy]
        at += wy
        for l in range(3):
            ephi[XO + halo(sx, l, wx), inner] = src[at : at + wy]
            at += wy
        edrift[0, edge, inner] = src[at : at + wy]
    for j, (_, sy) in enumerate(Y_DIRS):
        src, at, edge = ry.at[j], 0, YO + halo(sy, 0, wy)
        for i in links(1, sy):
            ext[i, 1 : 1 + wx, edge] = src[at : at + wx]
            at += wx
        ion0, ion1 = src[at : at + wx], src[at + wx : at + 2 * wx]
        eion[0, 1 : 1 + wx, edge] = ion0
        eion[1, 1 : 1 + wx, edge] = ion1
        at += 2 * wx
        echarge[XO : XO + wx, edge] = ion0 - ion1
        echarge[XO : XO + wx, YO + halo(sy, 1, wy)] = src[at : at + wx]
        at += wx
        for l in range(3):
            ephi[XO : XO + wx, YO + halo(sy, l, wy)] = src[at : at + wx]
            at += wx
        edrift[1, 1 : 1 + wx, edge] = src[at : at + wx]
    for j, (sx, sy) in enumerate(C_DIRS):
        src = rc.at[j]
        hx, hy = halo(sx, 0, wx), YO + halo(sy, 0, wy)
        ext[corner_link(sx, sy), 1 + hx, hy] = src[0]
        echarge[XO + hx, hy] = src[1]
        ephi[XO + hx, hy] = src[2]
        ephi[XO + halo(sx, 1, wx), hy] = src[3]
        ephi[XO + hx, YO + halo(sy, 1, wy)] = src[4]

    def velocity_plane(x, carry):
        read = []
        for i in range(19):
            sx, sy, sz = (int(c) for c in LATTICE[i])
            v = ext[i, 1 + x - sx, YO - sy : YO - sy + wy]
            read.append(v if sz == 0 else pltpu.roll(v, sz % depth, 1))
            read_out[i, x] = read[i]
        inverse = 1.0 / total_of(read)
        dens[x] = inverse
        for a in range(3):
            vels[a, x] = momentum(read, a) * inverse
        return carry

    lax.fori_loop(0, wx, velocity_plane, 0)

    def up(v):
        return jnp.where(lanes == depth - 1, 0.0, pltpu.roll(v, depth - 1, v.ndim - 1))

    def down(v):
        return jnp.where(lanes == 0, 0.0, pltpu.roll(v, 1, v.ndim - 1))

    def sweep(old, new, rim):
        lo, n = YO - rim, wy + 2 * rim

        def plane(t, carry):
            x = XO - rim + t
            mid = old[x, lo : lo + n]
            around = old[x + 1, lo : lo + n] + old[x - 1, lo : lo + n]
            around = around + (old[x, lo + 1 : lo + n + 1] + old[x, lo - 1 : lo + n - 1])
            around = around + (up(mid) + down(mid))
            new[x, lo : lo + n] = (around + kappa_charge * echarge[x, lo : lo + n]) / 6.0
            return carry

        lax.fori_loop(0, wx + 2 * rim, plane, 0)

    sweep(ephi, ephi1, 2)
    sweep(ephi1, ephi2, 1)

    def ion_plane(x, carry):
        flags = flags_ref[x]
        bit = lambda b: ((flags >> b) & 1).astype(F32)
        opened = [bit(b) for b in range(6)]
        phi = ephi2[XO + x, inner]
        phi_out[x] = phi
        phi_low = [ephi2[XO + x - 1, inner], ephi2[XO + x, YO - 1 : YO - 1 + wy]]
        phi_high = [ephi2[XO + x + 1, inner], ephi2[XO + x, YO + 1 : YO + 1 + wy]]
        phi_z_low, phi_z_high = pltpu.roll(phi, 1, 1), pltpu.roll(phi, depth - 1, 1)
        drift = [drift_ref[a, x] for a in range(3)]
        drift_low = [edrift[0, x, inner], edrift[1, 1 + x, YO - 1 : YO - 1 + wy]]
        drift_high = [edrift[0, x + 2, inner], edrift[1, 1 + x, YO + 1 : YO + 1 + wy]]
        drift_z_low = pltpu.roll(drift[2], 1, 1)

        def flux(lo_ion, hi_ion, lo_phi, hi_phi, lo_drift, hi_drift, gate, s):
            middle = 0.5 * (lo_ion + hi_ion)
            diffusive = -diffusion[s] * (
                (hi_ion - lo_ion) + valence[s] * middle * (hi_phi - lo_phi)
            )
            return gate * (diffusive + 0.5 * (lo_drift + hi_drift) * middle)

        both = []
        for s in range(2):
            ion = eion[s, 1 + x, inner]
            both.append(ion)
            ion_low = [eion[s, x, inner], eion[s, 1 + x, YO - 1 : YO - 1 + wy]]
            ion_high = [eion[s, x + 2, inner], eion[s, 1 + x, YO + 1 : YO + 1 + wy]]
            divergence = 0.0
            for a in range(2):
                entering = flux(
                    ion_low[a], ion, phi_low[a], phi, drift_low[a], drift[a], opened[2 * a], s
                )
                leaving = flux(
                    ion, ion_high[a], phi, phi_high[a], drift[a], drift_high[a], opened[2 * a + 1], s
                )
                divergence = divergence + (leaving - entering)
            entering = flux(
                pltpu.roll(ion, 1, 1), ion, phi_z_low, phi, drift_z_low, drift[2], opened[4], s
            )
            divergence = divergence + (pltpu.roll(entering, depth - 1, 1) - entering)
            ions_out[s, x] = ion - divergence
        charge = both[0] - both[1]

        field_x = (phi_low[0] - phi_high[0]) * 0.5
        field_y = (phi_low[1] - phi_high[1]) * 0.5
        field_z = (
            jnp.where(lanes == 0, 0.0, phi_z_low) - jnp.where(lanes == depth - 1, 0.0, phi_z_high)
        ) * 0.5
        scale = tau_relax * charge * dens[x]
        for a, e in enumerate((field_x, field_y, field_z)):
            shifted_out[a, x] = vels[a, x] + scale * e
        return carry

    lax.fori_loop(0, wx, ion_plane, 0)

    for copy in spheres:
        copy.wait()
    for n, (ref, (sx, sy)) in enumerate(zip([own] + eight(bxr, byr, bcr), [(0, 0)] + DIRS)):
        _, nx, tx = bead_span_x(sx, wx)
        _, ny, ty = bead_span_y(sy, wy)
        marks[n] = ref[0:8]
        for x in range(nx):
            held[n, tx + x, ty : ty + ny] = ref[8 + x * ny : 8 + (x + 1) * ny]
    reach = []
    for n in range(9):
        z = marks[n, 4:5].astype(jnp.int32)
        level = lax.broadcasted_iota(jnp.int32, (depth, 128), 0)
        reach.append(jnp.where(level == z, 1.0, 0.0).astype(BF16))

    parts = split3(vels[...].reshape(3 * rows, depth))
    for n in range(9):
        sampled = total_of(
            [lax.dot_general(p, reach[n], (((1,), (0,)), ((), ())), preferred_element_type=F32)
             for p in parts]
        )
        block = held[n].reshape(rows, 128)
        for k in range(3):
            part[n, k : k + 1] = jnp.sum(
                block * sampled[k * rows : (k + 1) * rows], axis=0, keepdims=True
            )
        part[n, 3:8] = jnp.zeros((5, 128), F32)
    backs = send_all(
        shape, [part.at[d + 1] for d in range(8)], [got.at[d] for d in range(8)],
        send.at[2], recv.at[2], -1,
    )

    for n in range(9):
        block = held[n].reshape(rows, 128)
        for k in range(4):
            for p, piece in enumerate(split3(block * marks[n, k : k + 1])):
                bead_rows[p, k * rows : (k + 1) * rows, n * 128 : (n + 1) * 128] = piece
    everywhere = jnp.concatenate(reach, 1)
    spread = total_of([dot_t(bead_rows[p], everywhere) for p in range(3)])
    pushes[...] = spread.reshape(4, wx, wy, depth)
    scale = (tau_relax * friction) * dens[...]
    for a in range(3):
        shifted_out[a] += scale * (pushes[a] - pushes[3] * vels[a])

    for copy in backs:
        copy.wait()
    whole = total_of([part[0]] + [got[d] for d in range(8)])
    group = lax.broadcasted_iota(jnp.int32, (8, 128), 1) // 16
    for s in range(2):
        m = [
            jnp.sum(jnp.where(group == 4 * s + q, whole, 0.0), axis=1, keepdims=True)
            for q in range(4)
        ]
        mean = [m[0][k : k + 1] for k in range(3)]
        lev = [[m[1 + a][k : k + 1] for k in range(3)] for a in range(3)]
        turned = [lev[1][2] - lev[2][1], lev[2][0] - lev[0][2], lev[0][1] - lev[1][0]]
        for k, t in enumerate(mean + turned):
            kick_ref[s : s + 1, k : k + 1] = (known[k][s : s + 1] - t) * (-friction / nb)


def second_kernel(
    read_ref, shifted_ref, flags_ref, ions_ref, phi_ref, kick_ref,
    pops_out, ions_out, phi_out, kick_out,
):
    kick_out[...] = kick_ref[...]

    def collide_plane(x, carry):
        phi_out[x] = phi_ref[x]
        for s in range(2):
            ions_out[s, x] = ions_ref[s, x]
        solid = ((flags_ref[x] >> 6) & 1) == 1
        read = [read_ref[i, x] for i in range(19)]
        density = total_of(read)
        shifted = [shifted_ref[a, x] for a in range(3)]
        base = 1.0 - 1.5 * (
            shifted[0] * shifted[0] + shifted[1] * shifted[1] + shifted[2] * shifted[2]
        )
        scaled = [w * density * (1.0 / tau_relax) for w in (1.0 / 3.0, 1.0 / 18.0, 1.0 / 36.0)]
        keep = 1.0 - 1.0 / tau_relax
        pops_out[0, x] = jnp.where(solid, read[0], keep * read[0] + scaled[0] * base)
        for i in range(1, 19, 2):
            along = 0.0
            for a in range(3):
                if LATTICE[i][a] != 0:
                    along = along + float(LATTICE[i][a]) * shifted[a]
            even = base + 4.5 * along * along
            odd = 3.0 * along
            scale = scaled[1] if i < 7 else scaled[2]
            pops_out[i, x] = jnp.where(
                solid, read[i + 1], keep * read[i] + scale * (even + odd)
            )
            pops_out[i + 1, x] = jnp.where(
                solid, read[i], keep * read[i + 1] + scale * (even - odd)
            )
        return carry

    lax.fori_loop(0, phi_ref.shape[0], collide_plane, 0)


def local(
    shape, populations, ion_density, potential, node_flags, colloid_count, colloid_centre,
    colloid_velocity, colloid_spin, bead_cell, bead_frac, bead_weight,
):
    wx, wy, depth = potential.shape
    kp = -(-bead_cell.shape[3] // 256) * 256
    vmem = pl.BlockSpec(memory_space=pltpu.VMEM)
    smem = pl.BlockSpec(memory_space=pltpu.SMEM)
    array = lambda *dims: jax.ShapeDtypeStruct(dims, F32)
    mem = lambda *dims: pltpu.VMEM(dims, F32)
    by_slot = lambda a: jnp.transpose(a, (1, 2, 3, 0)).reshape(a.shape[3], a.shape[0])
    tall, wide, far = wy + 2 * YO, wx + 2, wx + 2 * XO
    slabs = [mem(2, 12 * wy, depth), mem(2, 12 * wx, depth), mem(4, 8, depth)]
    balls = [mem(2, 8 + RADIUS * wy, 128), mem(2, 8 + wx * 8, 128), mem(4, 8 + RADIUS * 8, 128)]
    read, shifted, ions, phi, kick = pl.pallas_call(
        functools.partial(first_kernel, shape),
        out_shape=[
            array(*populations.shape), array(3, wx, wy, depth), array(*ion_density.shape),
            array(*potential.shape), array(2, 6),
        ],
        in_specs=[smem] * 4 + [vmem] * 7,
        out_specs=[vmem] * 5,
        scratch_shapes=slabs + slabs + balls + balls + [
            mem(8 + wx * wy, 128),
            mem(3, wx, wy, depth),
            mem(5, 2, kp),
            mem(6, 2, kp),
            mem(SIDE + 2 * (wx - 1), tall, 192),
            mem((wx + 2 * RADIUS) * tall, 128),
            mem(19, wide, tall, depth),
            mem(2, wide, tall, depth),
            mem(far, tall, depth),
            mem(2, wide, tall, depth),
            mem(far, tall, depth),
            mem(far, tall, depth),
            mem(far, tall, depth),
            mem(9, wx, wy, 128),
            mem(9, 8, 128),
            pltpu.VMEM((3, 4 * wx * wy, 9 * 128), BF16),
            mem(4, wx, wy, depth),
            mem(3, wx, wy, depth),
            mem(wx, wy, depth),
            mem(9, 8, 128),
            mem(8, 8, 128),
            pltpu.SemaphoreType.DMA((3, 8)),
            pltpu.SemaphoreType.DMA((3, 8)),
        ],
        compiler_params=pltpu.CompilerParams(collective_id=0, has_side_effects=True),
    )(
        colloid_count, by_slot(colloid_centre), by_slot(colloid_velocity), by_slot(colloid_spin),
        bead_cell, bead_frac, bead_weight, populations, ion_density, potential, node_flags,
    )
    pops_next, ions_next, phi_next, kick = pl.pallas_call(
        second_kernel,
        out_shape=[
            array(*populations.shape), array(*ion_density.shape), array(*potential.shape),
            array(2, 6),
        ],
        in_specs=[vmem] * 6,
        out_specs=[vmem] * 4,
    )(read, shifted, node_flags, ions, phi, kick)
    return pops_next, ions_next, phi_next, jnp.transpose(kick.reshape(1, 1, 2, 6), (3, 0, 1, 2))


def solution(mesh):
    in_specs = (
        P(None, "gx", "gy", None),
        P(None, "gx", "gy", None),
        P("gx", "gy", None),
        P("gx", "gy", None),
        P("gx", "gy"),
        P(None, "gx", "gy", None),
        P(None, "gx", "gy", None),
        P(None, "gx", "gy", None),
        P("gx", "gy", None, None),
        P(None, "gx", "gy", None, None),
        P("gx", "gy", None, None),
    )
    out_specs = (
        P(None, "gx", "gy", None),
        P(None, "gx", "gy", None),
        P("gx", "gy", None),
        P(None, "gx", "gy", None),
    )
    shape = (mesh.shape["gx"], mesh.shape["gy"])
    return jax.shard_map(
        functools.partial(local, shape), mesh=mesh, in_specs=in_specs, out_specs=out_specs,
        check_vma=False,
    )
```

time: 45.7 us -> 28 us (0.61)
  Pallas kernels: 38.7 us -> 26.5 us
  local copies, waits for them, and re-layouts: 5.29 us -> 0 us
    pallas_call x4 -> x2, Pallas kernels: 38.7 us -> 26.5 us  [the longest x1 23.5 us: local(): pl.pallas_call(functools.partial(first_kernel, shape), out_shape=[array(*...]
    unnamed x3 -> x0, local copies, waits for them, and re-layouts: 3.95 us -> none
    slice x1 -> x0, local copies, waits for them, and re-layouts: 1.34 us -> none  [local(): return (pops_next, ions_next, phi_next, kick[:, :, 0].reshape(6, 1, 1, 2))]
where the time goes in v2:
time: 28 us; the launch traced here: 27.8 us
  Pallas kernels  26.5 us (95%)
  between operations  1.29 us (5%)
    pallas_call x1, Pallas kernels, local(): pl.pallas_call(functools.partial(first_kernel, shape), out_shape=[array(*...  23.5 us
    pallas_call x1, Pallas kernels, local(): pl.pallas_call(second_kernel, out_shape=[array(*populations.shape), array...  3 us

profile of v2, /device:TPU:0, one launch (start us, length us, event | category | flops | bytes accessed | tf_op | source)
XLA Modules:
  0.0 27.8 jit_solution(15748751459490529190)
XLA Ops:
  1.3 23.5 %shard_map.138 = (f32[19,8,16,128]{3,2,1,0:T(8,128)}, f32[3,8,16,128]{3,2,1,0:T(8,128)}, f32[2,8,16,128]{3,2,1,0:T(8,128)}, f32[8,16,128]{2,1,0:T(8,128)}, f32[2,6]{1,0:T(2,128)}) custom-call(s32[1,1]{1,0:T(1,128)S(6)} %copy.15.count_ref, s32[2,3]{1,0:T(2,128)} %bitcast.12, f32[2,3]{1,0:T(2,128)} %bitcast.13, f32[2,3]{1,0:T(2,128)} %bitcast.14, ...), custom_call_target="tpu_custom_call" | custom-call | tf_op jit(solution)/shard_map/pallas_call | solution.py:575
  24.8 3.0 %shard_map.139 = (f32[19,8,16,128]{3,2,1,0:T(8,128)}, f32[2,8,16,128]{3,2,1,0:T(8,128)}, f32[8,16,128]{2,1,0:T(8,128)}, f32[2,6]{1,0:T(2,128)}) custom-call(f32[19,8,16,128]{3,2,1,0:T(8,128)} %get-tuple-element.13.read_ref, f32[3,8,16,128]{3,2,1,0:T(8,128)} %get-tuple-element.14.shifted_ref, s32[8,16,128]{2,1,0:T(8,128)} %flags_ref.3, ...), custom_call_target="tpu_custom_call" | custom-call | tf_op jit(solution)/shard_map/pallas_call | solution.py:613

commit v3 on v2

--- a/solution.py
+++ b/solution.py
@@ -150,7 +150,7 @@
     xs, ys, cs, rx, ry, rc, bxs, bys, bcs, bxr, byr, bcr, own,
     drift_ref, beads, codes, acc, field,
     ext, eion, echarge, edrift, ephi, ephi1, ephi2, held, marks, bead_rows, pushes, vels, dens,
-    part, got, send, recv,
+    part, got, streamed, send, recv, local_sem,
 ):
     wx, wy, depth = phi_ref.shape
     nb = cell_ref.shape[3]
@@ -166,52 +166,8 @@
     for sx, sy in DIRS:
         pl.semaphore_signal(barrier, inc=1, device_id=neighbour(shape, sx, sy), device_id_type=MESH)
 
-    def drift_plane(x, carry):
-        pops = [pops_ref[i, x] for i in range(19)]
-        inv = 1.0 / total_of(pops)
-        for a in range(3):
-            drift_ref[a, x] = momentum(pops, a) * inv
-        return carry
-
-    lax.fori_loop(0, wx, drift_plane, 0)
-
-    def charge_at(x, y):
-        return ions_ref[0, x, y] - ions_ref[1, x, y]
-
-    for j, (sx, _) in enumerate(X_DIRS):
-        out, at, edge = xs.at[j], 0, layer(sx, 0, wx)
-        parts = [pops_ref[i, edge] for i in links(0, sx)]
-        parts += [ions_ref[0, edge], ions_ref[1, edge], charge_at(layer(sx, 1, wx), slice(None))]
-        parts += [phi_ref[layer(sx, l, wx)] for l in range(3)] + [drift_ref[0, edge]]
-        for row in parts:
-            out[at : at + wy] = row
-            at += wy
-    for j, (_, sy) in enumerate(Y_DIRS):
-        out, at, edge = ys.at[j], 0, layer(sy, 0, wy)
-        parts = [pops_ref[i, :, edge] for i in links(1, sy)]
-        parts += [ions_ref[0, :, edge], ions_ref[1, :, edge]]
-        parts += [charge_at(slice(None), layer(sy, 1, wy))]
-        parts += [phi_ref[:, layer(sy, l, wy)] for l in range(3)] + [drift_ref[1, :, edge]]
-        for row in parts:
-            out[at : at + wx] = row
-            at += wx
-    for j, (sx, sy) in enumerate(C_DIRS):
-        out = cs.at[j]
-        ex, ey = layer(sx, 0, wx), layer(sy, 0, wy)
-        parts = [
-            pops_ref[corner_link(sx, sy), ex, ey],
-            charge_at(ex, ey),
-            phi_ref[ex, ey],
-            phi_ref[layer(sx, 1, wx), ey],
-            phi_ref[ex, layer(sy, 1, wy)],
-        ]
-        for at, row in enumerate(parts):
-            out[at] = row
-        out[5:8] = jnp.zeros((3, depth), F32)
-    pl.semaphore_wait(barrier, len(DIRS))
-    halos = send_all(
-        shape, eight(xs, ys, cs), eight(rx, ry, rc), send.at[0], recv.at[0], 1
-    )
+    load = pltpu.make_async_copy(pops_ref, ext.at[:, 1 : 1 + wx, inner], local_sem.at[0])
+    load.start()
 
     beads[...] = jnp.zeros_like(beads)
     beads[0, :, :nb] = cell_ref[0, 0].astype(F32)
@@ -304,6 +260,56 @@
     for ref, (sx, sy) in zip(eight(bxs, bys, bcs), DIRS):
         put_beads(ref, sx, sy)
     put_beads(own, 0, 0)
+
+    load.wait()
+
+    def drift_plane(x, carry):
+        pops = [ext[i, 1 + x, inner] for i in range(19)]
+        inv = 1.0 / total_of(pops)
+        for a in range(3):
+            drift_ref[a, x] = momentum(pops, a) * inv
+        return carry
+
+    lax.fori_loop(0, wx, drift_plane, 0)
+
+    def charge_at(x, y):
+        return ions_ref[0, x, y] - ions_ref[1, x, y]
+
+    for j, (sx, _) in enumerate(X_DIRS):
+        out, at, edge = xs.at[j], 0, layer(sx, 0, wx)
+        parts = [ext[i, 1 + edge, inner] for i in links(0, sx)]
+        parts += [ions_ref[0, edge], ions_ref[1, edge], charge_at(layer(sx, 1, wx), slice(None))]
+        parts += [phi_ref[layer(sx, l, wx)] for l in range(3)] + [drift_ref[0, edge]]
+        for row in parts:
+            out[at : at + wy] = row
+            at += wy
+    for j, (_, sy) in enumerate(Y_DIRS):
+        out, at, edge = ys.at[j], 0, layer(sy, 0, wy)
+        parts = [ext[i, 1 : 1 + wx, YO + edge] for i in links(1, sy)]
+        parts += [ions_ref[0, :, edge], ions_ref[1, :, edge]]
+        parts += [charge_at(slice(None), layer(sy, 1, wy))]
+        parts += [phi_ref[:, layer(sy, l, wy)] for l in range(3)] + [drift_ref[1, :, edge]]
+        for row in parts:
+            out[at : at + wx] = row
+            at += wx
+    for j, (sx, sy) in enumerate(C_DIRS):
+        out = cs.at[j]
+        ex, ey = layer(sx, 0, wx), layer(sy, 0, wy)
+        parts = [
+            ext[corner_link(sx, sy), 1 + ex, YO + ey],
+            charge_at(ex, ey),
+            phi_ref[ex, ey],
+            phi_ref[layer(sx, 1, wx), ey],
+            phi_ref[ex, layer(sy, 1, wy)],
+        ]
+        for at, row in enumerate(parts):
+            out[at] = row
+        out[5:8] = jnp.zeros((3, depth), F32)
+    pl.semaphore_wait(barrier, len(DIRS))
+    halos = send_all(
+        shape, eight(xs, ys, cs), eight(rx, ry, rc), send.at[0], recv.at[0], 1
+    )
+
     spheres = send_all(
         shape, eight(bxs, bys, bcs), eight(bxr, byr, bcr), send.at[1], recv.at[1], 1
     )
@@ -316,8 +322,6 @@
     twist = cross(lever, push)
     known = [jnp.sum(t, axis=1, keepdims=True) for t in push + twist]
 
-    for i in range(19):
-        ext[i, 1 : 1 + wx, inner] = pops_ref[i]
     for s in range(2):
         eion[s, 1 : 1 + wx, inner] = ions_ref[s]
     echarge[XO : XO + wx, inner] = ions_ref[0] - ions_ref[1]
@@ -373,7 +377,7 @@
             sx, sy, sz = (int(c) for c in LATTICE[i])
             v = ext[i, 1 + x - sx, YO - sy : YO - sy + wy]
             read.append(v if sz == 0 else pltpu.roll(v, sz % depth, 1))
-            read_out[i, x] = read[i]
+            streamed[i, x] = read[i]
         inverse = 1.0 / total_of(read)
         dens[x] = inverse
         for a in range(3):
@@ -381,6 +385,43 @@
         return carry
 
     lax.fori_loop(0, wx, velocity_plane, 0)
+
+    for copy in spheres:
+        copy.wait()
+    save = pltpu.make_async_copy(streamed, read_out, local_sem.at[1])
+    save.start()
+    for n, (ref, (sx, sy)) in enumerate(zip([own] + eight(bxr, byr, bcr), [(0, 0)] + DIRS)):
+        _, nx, tx = bead_span_x(sx, wx)
+        _, ny, ty = bead_span_y(sy, wy)
+        marks[n] = ref[0:8]
+        for x in range(nx):
+            held[n, tx + x, ty : ty + ny] = ref[8 + x * ny : 8 + (x + 1) * ny]
+    reach = []
+    for n in range(9):
+        z = marks[n, 4:5].astype(jnp.int32)
+        level = lax.broadcasted_iota(jnp.int32, (depth, 128), 0)
+        reach.append(jnp.where(level == z, 1.0, 0.0).astype(BF16))
+
+    parts = split3(vels[...].reshape(3 * rows, depth))
+    def partial_sums(n):
+        sampled = total_of(
+            [lax.dot_general(p, reach[n], (((1,), (0,)), ((), ())), preferred_element_type=F32)
+             for p in parts]
+        )
+        block = held[n].reshape(rows, 128)
+        for k in range(3):
+            part[n, k : k + 1] = jnp.sum(
+                block * sampled[k * rows : (k + 1) * rows], axis=0, keepdims=True
+            )
+        part[n, 3:8] = jnp.zeros((5, 128), F32)
+
+    for n in range(1, 9):
+        partial_sums(n)
+    backs = send_all(
+        shape, [part.at[d + 1] for d in range(8)], [got.at[d] for d in range(8)],
+        send.at[2], recv.at[2], -1,
+    )
+    partial_sums(0)
 
     def up(v):
         return jnp.where(lanes == depth - 1, 0.0, pltpu.roll(v, depth - 1, v.ndim - 1))
@@ -460,37 +501,6 @@
 
     lax.fori_loop(0, wx, ion_plane, 0)
 
-    for copy in spheres:
-        copy.wait()
-    for n, (ref, (sx, sy)) in enumerate(zip([own] + eight(bxr, byr, bcr), [(0, 0)] + DIRS)):
-        _, nx, tx = bead_span_x(sx, wx)
-        _, ny, ty = bead_span_y(sy, wy)
-        marks[n] = ref[0:8]
-        for x in range(nx):
-            held[n, tx + x, ty : ty + ny] = ref[8 + x * ny : 8 + (x + 1) * ny]
-    reach = []
-    for n in range(9):
-        z = marks[n, 4:5].astype(jnp.int32)
-        level = lax.broadcasted_iota(jnp.int32, (depth, 128), 0)
-        reach.append(jnp.where(level == z, 1.0, 0.0).astype(BF16))
-
-    parts = split3(vels[...].reshape(3 * rows, depth))
-    for n in range(9):
-        sampled = total_of(
-            [lax.dot_general(p, reach[n], (((1,), (0,)), ((), ())), preferred_element_type=F32)
-             for p in parts]
-        )
-        block = held[n].reshape(rows, 128)
-        for k in range(3):
-            part[n, k : k + 1] = jnp.sum(
-                block * sampled[k * rows : (k + 1) * rows], axis=0, keepdims=True
-            )
-        part[n, 3:8] = jnp.zeros((5, 128), F32)
-    backs = send_all(
-        shape, [part.at[d + 1] for d in range(8)], [got.at[d] for d in range(8)],
-        send.at[2], recv.at[2], -1,
-    )
-
     for n in range(9):
         block = held[n].reshape(rows, 128)
         for k in range(4):
@@ -503,6 +513,7 @@
     for a in range(3):
         shifted_out[a] += scale * (pushes[a] - pushes[3] * vels[a])
 
+    save.wait()
     for copy in backs:
         copy.wait()
     whole = total_of([part[0]] + [got[d] for d in range(8)])
@@ -566,6 +577,7 @@
     kp = -(-bead_cell.shape[3] // 256) * 256
     vmem = pl.BlockSpec(memory_space=pltpu.VMEM)
     smem = pl.BlockSpec(memory_space=pltpu.SMEM)
+    hbm = pl.BlockSpec(memory_space=pl.ANY)
     array = lambda *dims: jax.ShapeDtypeStruct(dims, F32)
     mem = lambda *dims: pltpu.VMEM(dims, F32)
     by_slot = lambda a: jnp.transpose(a, (1, 2, 3, 0)).reshape(a.shape[3], a.shape[0])
@@ -578,8 +590,8 @@
             array(*populations.shape), array(3, wx, wy, depth), array(*ion_density.shape),
             array(*potential.shape), array(2, 6),
         ],
-        in_specs=[smem] * 4 + [vmem] * 7,
-        out_specs=[vmem] * 5,
+        in_specs=[smem] * 4 + [vmem] * 3 + [hbm] + [vmem] * 3,
+        out_specs=[hbm] + [vmem] * 4,
         scratch_shapes=slabs + slabs + balls + balls + [
             mem(8 + wx * wy, 128),
             mem(3, wx, wy, depth),
@@ -602,8 +614,10 @@
             mem(wx, wy, depth),
             mem(9, 8, 128),
             mem(8, 8, 128),
+            mem(*populations.shape),
             pltpu.SemaphoreType.DMA((3, 8)),
             pltpu.SemaphoreType.DMA((3, 8)),
+            pltpu.SemaphoreType.DMA((2,)),
         ],
         compiler_params=pltpu.CompilerParams(collective_id=0, has_side_effects=True),
     )(

time: 28 us -> 25.1 us (0.90)
  Pallas kernels: 26.5 us -> 23.6 us
    pallas_call x1, Pallas kernels: 23.5 us -> 20.6 us  [local(): pl.pallas_call(functools.partial(first_kernel, shape), out_shape=[array(*...]
where the time goes in v3:
time: 25.1 us; the launch traced here: 24.9 us
  Pallas kernels  23.6 us (94%)
  between operations  1.29 us (5%)
    pallas_call x1, Pallas kernels, local(): pl.pallas_call(functools.partial(first_kernel, shape), out_shape=[array(*...  20.6 us
    pallas_call x1, Pallas kernels, local(): pl.pallas_call(second_kernel, out_shape=[array(*populations.shape), array...  3 us

profile of v3, /device:TPU:0, one launch (start us, length us, event | category | flops | bytes accessed | tf_op | source)
XLA Modules:
  0.0 24.9 jit_solution(6835211602897661859)
XLA Ops:
  1.3 20.6 %shard_map.138 = (f32[19,8,16,128]{3,2,1,0:T(8,128)}, f32[3,8,16,128]{3,2,1,0:T(8,128)}, f32[2,8,16,128]{3,2,1,0:T(8,128)}, f32[8,16,128]{2,1,0:T(8,128)}, f32[2,6]{1,0:T(2,128)}) custom-call(s32[1,1]{1,0:T(1,128)S(6)} %copy.15.count_ref, s32[2,3]{1,0:T(2,128)} %bitcast.12, f32[2,3]{1,0:T(2,128)} %bitcast.13, f32[2,3]{1,0:T(2,128)} %bitcast.14, ...), custom_call_target="tpu_custom_call" | custom-call | tf_op jit(solution)/shard_map/pallas_call | solution.py:587
  21.9 3.0 %shard_map.139 = (f32[19,8,16,128]{3,2,1,0:T(8,128)}, f32[2,8,16,128]{3,2,1,0:T(8,128)}, f32[8,16,128]{2,1,0:T(8,128)}, f32[2,6]{1,0:T(2,128)}) custom-call(f32[19,8,16,128]{3,2,1,0:T(8,128)} %get-tuple-element.13.read_ref, f32[3,8,16,128]{3,2,1,0:T(8,128)} %get-tuple-element.14.shifted_ref, s32[8,16,128]{2,1,0:T(8,128)} %flags_ref.3, ...), custom_call_target="tpu_custom_call" | custom-call | tf_op jit(solution)/shard_map/pallas_call | solution.py:627
